TPU v7x, 32 devices: a whole 2x2x4 slice. The times are simulated.
32 devices in a mesh: rows: 8 (over z, y), cols: 4 (over x, core).
Axes of the slice: x: 2, y: 2, z: 4, core: 2. Of those that a mesh axis runs over, the one named last changes fastest.
Arguments:
- samples: float32 [64, 32768], P('cols', 'rows')
- loadings: bfloat16 [256, 32768], P(None, 'rows')
- omega_tiles: float32 [320, 512, 512], P(('rows', 'cols')), may hold values from -0.18 to 0.18
- omega_diagonal: float32 [32768], P('rows'), may hold values from 0.5 to 2
- tile_rows: int32 [320], replicated, may hold values from 0 to 63, as said below
- tile_cols: int32 [320], replicated, may hold values from 0 to 63, as said below
Outputs:
- new_tiles: float32 [320, 512, 512], P(('rows', 'cols'))
- new_diagonal: float32 [32768], P('rows')
Inputs may be any that keep to these rules, and one draw needn't show every extreme that they name: Slot s belongs to group g = s // 40; tile_rows[s] lies between g * 8 and g * 8 + 7. A block row may hold any number of tiles, none included. `tile_cols`: of the 40 tiles of one group, at most 10 have column blocks in any one group h (blocks h * 8 to h * 8 + 7), and in every group exactly 10 have column blocks in some one group.
All inputs are finite; a program needn't handle non-finite values.
Results may differ from a plain program's by a relative error of at most 0.0003.
Values sent between devices are 32-bit elements; how exact they have to be, the bound alone decides.
No kernel may reach another device: no remote copies, remote signals or barrier semaphores. Data moves between devices by JAX's collectives and lax.ppermute only.
A program may use at most 64 MiB of HBM per device.

v0:
```python
import functools

import jax
import jax.numpy as jnp
from jax import lax
from jax.experimental import pallas as pl
from jax.experimental.pallas import tpu as pltpu
from jax.sharding import Mesh
from jax.sharding import PartitionSpec as P

step_size = 0.5
penalty = 0.02

ROWS = ("a", "u", "v")
COLS = ("x", "k")
PLANE = ("u", "v", "x")


def exchange_order(a_count):
    return [(da, dz) for da in reversed(range(a_count)) for dz in (1, 0)]


def plane_order(x_count):
    steps = [(du, dv, dx) for du in range(2) for dv in range(2) for dx in range(x_count)]
    return sorted(steps[1:], key=lambda step: -sum(part > 0 for part in step))


NT = (((1,), (1,)), ((), ()))
NN = (((1,), (0,)), ((), ()))


def dot(left, right, dims):
    return lax.dot_general(left, right, dims, preferred_element_type=jnp.float32)


def split(value, pieces):
    found = []
    for _ in range(pieces):
        piece = value.astype(jnp.bfloat16)
        found.append(piece)
        value = value - piece.astype(jnp.float32)
    return found


def table_kernel(sizes, place, tile_rows, tile_cols, after, row_local, is_diag, slot_index):
    x_count, blocks = sizes
    a, u, v, x, k = (place[at] for at in range(5))
    tile_dev = row_local.shape[0]

    def first_tile(u, v, x):
        return ((((a * 2 + u) * 2 + v) * x_count + x) * 2 + k) * tile_dev

    mine = first_tile(u, v, x)
    for at in range(tile_dev):
        row, col = tile_rows[mine + at], tile_cols[mine + at]
        row_local[at] = row - ((a * 2 + u) * 2 + v) * blocks
        is_diag[at] = jnp.where(row == col, 1, 0)
    a_count = tile_cols.shape[0] // (8 * x_count * tile_dev)
    peer = 0
    for du in range(2):
        for dv in range(2):
            for dx in range(x_count):
                theirs = first_tile(u ^ du, v ^ dv, lax.rem(x + dx, x_count))
                for at in range(tile_dev):
                    col = tile_cols[theirs + at]
                    group = col // blocks
                    da = lax.rem(a + a_count - group // 4, a_count)
                    part = (da * 2 + (((group // 2) % 2) ^ u)) * 2 + ((group % 2) ^ k)
                    slot_index[peer * tile_dev + at] = part * blocks + col % blocks
                peer += 1


def score_kernel(samples, loadings, out, held_samples, held, sem):
    rows, variables = samples.shape
    chunks = sem.shape[0] - 1
    width = variables // chunks
    whole = pltpu.make_async_copy(samples, held_samples, sem.at[chunks])
    whole.start()
    copies = [
        pltpu.make_async_copy(
            loadings.at[:, at * width : (at + 1) * width],
            held.at[:, at * width : (at + 1) * width],
            sem.at[at],
        )
        for at in range(chunks)
    ]
    for copy in copies:
        copy.start()
    whole.wait()
    found = None
    for at, copy in enumerate(copies):
        here = slice(at * width, (at + 1) * width)
        pieces = jnp.concatenate(split(held_samples[:, here], 3), 0)
        copy.wait()
        term = dot(pieces, held[:, here], NT)
        found = term if found is None else found + term
    value = (found[2 * rows :] + found[rows : 2 * rows]) + found[:rows]
    for copy in range(out.shape[0]):
        out[copy] = value


def residual_kernel(place, scores, samples, loadings, after, whole, first, second):
    rows, variables = samples.shape
    half = rows // 2
    value = scores[0]
    for source in range(1, scores.shape[0]):
        value = value + scores[source]
    pieces = jnp.concatenate(split(value, 3), 0)
    upper = place[1] == 1
    width = variables // 4
    for at in range(0, variables, width):
        here = slice(at, at + width)
        fitted = dot(pieces, loadings[:, here], NN)
        value = samples[:, here] - ((fitted[2 * rows :] + fitted[rows : 2 * rows]) + fitted[:rows])
        low, high = value[:half], value[half:]
        near = jnp.where(upper, high, low)
        far = jnp.where(upper, low, high)
        whole[:half, here] = near
        whole[half:, here] = far
        first[:, here] = near
        second[:, here] = far


def gather_kernel(count, peers, index, *refs):
    sources, outs, held = refs[:count], refs[-1 - peers : -1], refs[-1]
    for at, source in enumerate(sources):
        held[at] = source[...]
    tile_dev, _, width = outs[0].shape
    blocks = held.shape[2] // width
    for peer, out in enumerate(outs):
        for at in range(tile_dev):
            code = index[peer * tile_dev + at]
            start = pl.multiple_of((code % blocks) * width, width)
            out[at] = held[code // blocks, :, pl.ds(start, width)]


def block_of(routed, at):
    return jnp.concatenate([part[at] for part in routed], 0)


def masked(tile, is_diag):
    size = tile.shape[0]
    row = lax.broadcasted_iota(jnp.int32, (size, size), 0)
    col = lax.broadcasted_iota(jnp.int32, (size, size), 1)
    return jnp.where((row == col) & (is_diag == 1), 0.0, tile)


def fetch_tiles(tiles, held, sem):
    copies = [
        pltpu.make_async_copy(tiles.at[at], held.at[at], sem.at[at]) for at in range(tiles.shape[0])
    ]
    for copy in copies:
        copy.start()


def tile_kernel(is_diag, tiles, after, high, low, held, sem):
    fetch_tiles(tiles, held, sem)

    def convert(at, carry):
        pltpu.make_async_copy(tiles.at[at], held.at[at], sem.at[at]).wait()
        high[at], low[at] = split(masked(held[at], is_diag[at]), 2)
        return carry

    lax.fori_loop(0, tiles.shape[0], convert, 0)


def product_kernel(x_count, row_local, place, tile_hi, tile_lo, *refs):
    routed, (keep, give, total) = refs[:-3], refs[-3:]
    blocks, samples, block = total.shape
    total[...] = jnp.zeros_like(total)

    def multiply(at, carry):
        source_hi, source_lo = split(block_of(routed, at), 2)
        stacked = dot(jnp.concatenate([source_hi, source_lo], 0), tile_hi[at], NT)
        product = stacked[:samples] + (stacked[samples:] + dot(source_hi, tile_lo[at], NT))
        total[row_local[at]] += product
        return carry

    lax.fori_loop(0, tile_hi.shape[0], multiply, 0)
    half = keep.shape[1] // 2
    for out, core in ((keep, place[4]), (give, 1 - place[4])):
        for dx in range(x_count):
            for du in range(2):
                source = (du * 2 + (place[2] ^ core)) * x_count + (x_count - dx) % x_count
                start = pl.multiple_of(source * half, half)
                for at in range(blocks):
                    out[dx, du * half : (du + 1) * half, at * block : (at + 1) * block] = total[
                        at, pl.ds(start, half), :
                    ]


def applied_kernel(count, *refs):
    keep, got, residual, diagonal = refs[:4]
    arrived = refs[4 : 4 + count]
    whole, first, second = refs[4 + count :]
    half = first.shape[0]
    value = keep[0] + got[0]
    for other in arrived:
        value = value + other[...]
    value = value + diagonal[...] * residual[...]
    whole[...] = value
    first[...] = value[:half]
    second[...] = value[half:]


def place_rows(x_count, place, parts, rows):
    half = parts[0].shape[0] // 2
    for dk in range(2):
        for dx in range(x_count):
            for du in range(2):
                target = (du * 2 + (place[2] ^ place[4] ^ dk)) * x_count + dx
                start = pl.multiple_of(target * half, half)
                rows[pl.ds(start, half)] = parts[dk * x_count + dx][du * half : (du + 1) * half]


def left_operand(rows, scale):
    high, low = split((rows * scale).T, 2)
    return jnp.concatenate([high, high, low], 1)


def right_operand(rows):
    high, low = split(rows, 2)
    return jnp.concatenate([high, low, high], 0)


def row_kernel(x_count, scale, place, after, *refs):
    parts, (rows, left) = refs[:-2], refs[-2:]
    place_rows(x_count, place, parts, rows)
    block = left.shape[1]
    for at in range(left.shape[0]):
        left[at] = left_operand(rows[:, at * block : (at + 1) * block], scale)


def first_kernel(x_count, scale, row_local, place, tiles, diagonal, resid_rows, after, *refs):
    inputs, (partial, new_diagonal, rows, left, sem) = refs[:-5], refs[-5:]
    parts, routed = inputs[: 2 * x_count], inputs[2 * x_count :]
    fetch_tiles(tiles, partial, sem)
    samples = rows.shape[0]
    block = left.shape[1]
    place_rows(x_count, place, parts, rows)
    for at in range(left.shape[0]):
        left[at] = left_operand(rows[:, at * block : (at + 1) * block], scale)
    stat = jnp.sum(rows[...] * resid_rows[...], axis=0, keepdims=True) / samples
    new_diagonal[...] = diagonal[...] - step_size * (stat - 1.0 / diagonal[...])

    def subtract(at, carry):
        right = right_operand(block_of(routed, at))
        term = dot(left[row_local[at]], right, NN)
        pltpu.make_async_copy(tiles.at[at], partial.at[at], sem.at[at]).wait()
        partial[at] = partial[at] + term
        return carry

    lax.fori_loop(0, tiles.shape[0], subtract, 0)


def last_kernel(row_local, is_diag, left, partial, *refs):
    routed, (new_tiles, held, sem) = refs[:-3], refs[-3:]
    bound = step_size * penalty

    def finish(at, carry):
        right = right_operand(block_of(routed, at))
        stepped = partial[at] + dot(left[row_local[at]], right, NN)
        held[at] = stepped - jnp.clip(stepped, -bound, bound)

        @pl.when(is_diag[at] == 1)
        def _():
            held[at] = masked(held[at], 1)

        pltpu.make_async_copy(held.at[at], new_tiles.at[at], sem.at[at]).start()
        return carry

    lax.fori_loop(0, partial.shape[0], finish, 0)
    for at in range(partial.shape[0]):
        pltpu.make_async_copy(held.at[at], new_tiles.at[at], sem.at[at]).wait()


def per_device(samples, loadings, omega_tiles, omega_diagonal, tile_rows, tile_cols):
    f32 = jnp.float32
    a_count, x_count = lax.axis_size("a"), lax.axis_size("x")
    row_count, col_count = 4 * a_count, 2 * x_count
    a, u, v, x, k = (lax.axis_index(name) for name in ROWS + COLS)
    sample_dev, var_dev = samples.shape
    half = sample_dev // 2
    sample_all = sample_dev * col_count
    factors = loadings.shape[0]
    tile_dev, block_size = omega_tiles.shape[:2]
    blocks_dev = var_dev // block_size
    plane = 4 * x_count
    hbm = pl.BlockSpec(memory_space=pltpu.HBM)
    vmem = pl.BlockSpec(memory_space=pltpu.VMEM)

    def cost(flops, moved):
        return pl.CostEstimate(flops=flops, bytes_accessed=moved, transcendentals=0)

    shape = lambda *dims: jax.ShapeDtypeStruct(dims, f32)

    place = jnp.stack([a, u, v, x, k]).astype(jnp.int32)

    def permute(value, names, target):
        sizes = [lax.axis_size(name) for name in names]

        def flat(coords):
            at = 0
            for coord, size in zip(coords, sizes):
                at = at * size + coord
            return at

        def coords_of(at):
            coords = []
            for size in reversed(sizes):
                coords.append(at % size)
                at //= size
            return tuple(reversed(coords))

        total = 1
        for size in sizes:
            total *= size
        return lax.ppermute(
            value, names, [(at, flat(target(*coords_of(at)))) for at in range(total)]
        )

    def swap_core(value):
        return permute(value, ("k",), lambda k: (1 - k,))

    def shift_x(value, dx):
        return permute(value, ("x",), lambda x: ((x + dx) % x_count,))

    def call(kernel, outs, operands, scratch=(), limit=24, estimate=None):
        arrays, specs = [], []
        for array, spec in operands:
            if spec is vmem:
                array = pltpu.with_memory_space_constraint(array, pltpu.VMEM)
            if spec is hbm:
                array = pltpu.with_memory_space_constraint(array, pltpu.HBM)
            arrays.append(array)
            specs.append(spec)
        return pl.pallas_call(
            kernel,
            out_shape=[out for out, _ in outs],
            in_specs=specs,
            out_specs=[spec for _, spec in outs],
            scratch_shapes=list(scratch),
            compiler_params=pltpu.CompilerParams(vmem_limit_bytes=limit * 1024 * 1024),
            cost_estimate=estimate,
        )(*arrays)

    def chip(dims, dtype=f32):
        return (pltpu.VMEM(dims, dtype), vmem)

    smem = pl.BlockSpec(memory_space=pltpu.SMEM)
    bf16 = jnp.bfloat16
    diagonal = omega_diagonal.reshape(1, var_dev)
    depth = 3 * sample_all
    tile_elements = tile_dev * block_size * block_size
    tile_sem = pltpu.SemaphoreType.DMA((tile_dev,))
    tile_shape = omega_tiles.shape
    scale = -step_size * 0.5 / sample_all
    field_outs = [chip((sample_dev, var_dev)), chip((half, var_dev)), chip((half, var_dev))]

    score_copies, held_samples, held_loadings = call(
        score_kernel,
        [
            chip((row_count, sample_dev, factors)),
            chip(samples.shape),
            chip(loadings.shape, bf16),
        ],
        [(samples, hbm), (loadings, hbm)],
        [pltpu.SemaphoreType.DMA((5,))],
    )
    score_terms = lax.all_to_all(score_copies, ROWS, 0, 0, tiled=True)
    row_local, is_diag, slot_index = call(
        functools.partial(table_kernel, (x_count, blocks_dev)),
        [
            (jax.ShapeDtypeStruct((count,), jnp.int32), smem)
            for count in (tile_dev, tile_dev, plane * tile_dev)
        ],
        [(place, smem), (tile_rows, smem), (tile_cols, smem), (score_copies, vmem)],
    )
    residual, resid_near, resid_far = call(
        residual_kernel,
        field_outs,
        [
            (place, smem),
            (score_terms, vmem),
            (held_samples, vmem),
            (held_loadings, vmem),
            (slot_index, smem),
        ],
    )

    def own_rows(whole):
        parts = [whole]
        for dx in range(1, x_count):
            parts.append(shift_x(whole, dx))
        return parts + [swap_core(part) for part in parts]

    def route(near, far, whole):
        held = [None] * (2 * a_count)
        for da, dz in exchange_order(a_count):
            held[da * 2 + dz] = permute(
                far if dz else near,
                ("a", "u", "v", "k"),
                lambda a, u, v, k: ((a + da) % a_count, u ^ dz, k, v),
            )
        beside = own_rows(whole)
        sources = []
        for part in held:
            sources += [part, swap_core(part)]
        slots = call(
            functools.partial(gather_kernel, len(sources), plane),
            [chip((tile_dev, half, block_size))] * plane,
            [(slot_index, smem)] + [(part, vmem) for part in sources + beside],
            [pltpu.VMEM((len(sources), half, var_dev), f32)],
        )
        return slots, beside

    def deliver(slots):
        routed = list(slots)
        for du, dv, dx in plane_order(x_count):
            at = (du * 2 + dv) * x_count + dx
            routed[at] = permute(
                slots[at], PLANE, lambda u, v, x: (u ^ du, v ^ dv, (x + dx) % x_count)
            )
        return routed

    resid_slots, resid_parts = route(resid_near, resid_far, residual)
    routed_resid = deliver(resid_slots)
    tiles_hi, tiles_lo = call(
        tile_kernel,
        [chip(tile_shape, bf16), chip(tile_shape, bf16)],
        [(is_diag, smem), (omega_tiles, hbm), (resid_slots[0], vmem)],
        [pltpu.VMEM(tile_shape, f32), tile_sem],
        estimate=cost(0, 8 * tile_elements),
    )
    resid_rows, resid_left = call(
        functools.partial(row_kernel, x_count, scale),
        [chip((sample_all, var_dev)), chip((blocks_dev, block_size, depth), bf16)],
        [(place, smem), (resid_slots[0], vmem)] + [(part, vmem) for part in resid_parts],
        estimate=cost(0, 16 * sample_all * var_dev),
    )

    keep, give = call(
        functools.partial(product_kernel, x_count),
        [chip((x_count, sample_dev, var_dev))] * 2,
        [
            (row_local, smem),
            (place, smem),
            (tiles_hi, vmem),
            (tiles_lo, vmem),
        ]
        + [(part, vmem) for part in routed_resid],
        [pltpu.VMEM((blocks_dev, sample_all, block_size), f32)],
    )
    got = swap_core(give)
    arrived = [shift_x(keep[dx] + got[dx], dx) for dx in range(1, x_count)]
    applied, applied_near, applied_far = call(
        functools.partial(applied_kernel, len(arrived)),
        field_outs,
        [(part, vmem) for part in (keep, got, residual, diagonal, *arrived)],
    )

    applied_slots, applied_parts = route(applied_near, applied_far, applied)
    routed_applied = deliver(applied_slots)
    partial, new_diagonal = call(
        functools.partial(first_kernel, x_count, scale),
        [chip(tile_shape), (shape(1, var_dev), vmem)],
        [
            (row_local, smem),
            (place, smem),
            (omega_tiles, hbm),
            (diagonal, vmem),
            (resid_rows, vmem),
            (applied_slots[0], vmem),
        ]
        + [(part, vmem) for part in applied_parts + routed_resid],
        [
            pltpu.VMEM((sample_all, var_dev), f32),
            pltpu.VMEM((blocks_dev, block_size, depth), bf16),
            tile_sem,
        ],
        estimate=cost(2 * depth * tile_elements, 16 * tile_elements),
    )
    (new_tiles,) = call(
        last_kernel,
        [(shape(*tile_shape), hbm)],
        [
            (row_local, smem),
            (is_diag, smem),
            (resid_left, vmem),
            (partial, vmem),
        ]
        + [(part, vmem) for part in routed_applied],
        [pltpu.VMEM(tile_shape, f32), tile_sem],
    )
    return new_tiles, new_diagonal.reshape(var_dev)


def solution(mesh):
    rows, cols = mesh.shape["rows"], mesh.shape["cols"]
    fine = Mesh(mesh.devices.reshape(rows // 4, 2, 2, cols // 2, 2), ROWS + COLS)
    placed = (
        P(COLS, ROWS),
        P(None, ROWS),
        P(ROWS + COLS, None, None),
        P(ROWS),
        P(),
        P(),
    )
    return jax.shard_map(
        per_device,
        mesh=fine,
        in_specs=placed,
        out_specs=(P(ROWS + COLS, None, None), P(ROWS)),
        check_vma=False,
    )
```

profile of v0, /device:TPU:0, one launch (start us, length us, event | category | flops | bytes accessed | tf_op | source)
XLA Modules:
  0.0 121.0 jit_solution(7834669586244112593)
XLA Ops:
  0.6 3.4 %shard_map.77 = (f32[8,16,256]{2,1,0:T(8,128)}, f32[16,4096]{1,0:T(8,128)S(1)}, bf16[256,4096]{1,0:T(8,128)(2,1)S(1)}) custom-call(f32[16,4096]{1,0:T(8,128)} %samples.1, bf16[256,4096]{1,0:T(8,128)(2,1)} %loadings.1), custom_call_target="tpu_custom_call" | custom-call | tf_op jit(solution)/shard_map/pallas_call | solution.py:337
  4.0 7.3 %all-to-all-start = ((f32[8,16,256]{2,1,0:T(8,128)}), f32[8,16,256]{2,1,0:T(8,128)S(1)}, u32[]{:S(2)}, u32[]{:S(2)}) async-start(f32[8,16,256]{2,1,0:T(8,128)} %get-tuple-element.38.after), calls=%async_computation | async-start | bytes 262144 | tf_op jit(solution)/shard_map/all_to_all | solution.py:370
  11.3 0.1 stack.23.place
  11.4 0.7 copy-done.1
  12.1 0.7 copy-done.2
  12.8 3.2 %shard_map.78 = (s32[10]{0:T(128)S(1)}, s32[10]{0:T(128)S(1)}, s32[80]{0:T(128)S(1)}) custom-call(s32[5]{0:T(128)S(1)} %stack.23.place, s32[320]{0:T(512)S(1)} %copy-done.1, s32[320]{0:T(512)S(1)} %copy-done.2, f32[8,16,256]{2,1,0:T(8,128)} %get-tuple-element.38.after), custom_call_target="tpu_custom_call" | custom-call | tf_op jit(solution)/shard_map/pallas_call | solution.py:337
  15.9 2.7 %all-to-all-done.scores = f32[8,16,256]{2,1,0:T(8,128)S(1)} async-done(((f32[8,16,256]{2,1,0:T(8,128)}), f32[8,16,256]{2,1,0:T(8,128)S(1)}, u32[]{:S(2)}, u32[]{:S(2)}) %all-to-all-start) | async-done | bytes 131104 | tf_op jit(solution)/shard_map/all_to_all | solution.py:370
  18.7 1.0 shard_map.79
  19.6 1.6 %collective-permute-start.8 = (f32[16,4096]{1,0:T(8,128)S(1)}, f32[16,4096]{1,0:T(8,128)S(1)}, u32[]{:S(2)}, u32[]{:S(2)}) collective-permute-start(f32[16,4096]{1,0:T(8,128)S(1)} %get-tuple-element.46.refs_8_.refs_0_.refs_2_), channel_id=1, source_target_pairs={{0,2},{2,0},{1,3},{3,1},{4,6},{6,4},{5,7},{7,5},{8,10},{10,8},{9,1... | collective-permute-start | bytes 786440 | tf_op jit(solution)/shard_map/ppermute | solution.py:318
  21.2 0.4 collective-permute-start.4
  21.6 0.7 collective-permute-start
  22.3 1.9 %collective-permute-start.6 = (f32[8,4096]{1,0:T(8,128)S(1)}, f32[8,4096]{1,0:T(8,128)S(1)}, u32[]{:S(2)}, u32[]{:S(2)}) collective-permute-start(f32[8,4096]{1,0:T(8,128)S(1)} %get-tuple-element.45), channel_id=1, source_target_pairs={{0,24},{1,28},{4,25},{5,29},{8,16},{9,20},{12,17},{13,21},{16,8},{... | collective-permute-start | bytes 393224 | tf_op jit(solution)/shard_map/ppermute | solution.py:318
  24.2 1.3 %collective-permute-start.2 = (f32[8,4096]{1,0:T(8,128)S(1)}, f32[8,4096]{1,0:T(8,128)S(1)}, u32[]{:S(2)}, u32[]{:S(2)}) collective-permute-start(f32[8,4096]{1,0:T(8,128)S(1)} %get-tuple-element.45), channel_id=1, source_target_pairs={{0,8},{1,12},{4,9},{5,13},{8,0},{9,4},{12,1},{13,5},{16,24},{17,28... | collective-permute-start | bytes 393224 | tf_op jit(solution)/shard_map/ppermute | solution.py:318
  25.4 8.1 %collective-permute-done.4.refs_4_ = f32[8,4096]{1,0:T(8,128)S(1)} collective-permute-done((f32[8,4096]{1,0:T(8,128)S(1)}, f32[8,4096]{1,0:T(8,128)S(1)}, u32[]{:S(2)}, u32[]{:S(2)}) %collective-permute-start.4) | collective-permute-done | bytes 131104 | tf_op jit(solution)/shard_map/ppermute | solution.py:318
  33.5 0.0 collective-permute-start.5
  33.5 0.0 collective-permute-done.refs_0_
  33.5 0.5 collective-permute-start.9
  34.0 0.0 collective-permute-done.8.refs_9_.refs_1_
  34.1 0.1 collective-permute-start.10
  34.1 0.4 collective-permute-start.1
  34.6 1.0 collective-permute-done.2.refs_2_
  35.6 0.5 collective-permute-start.3
  36.1 0.8 collective-permute-done.7.refs_7_
  36.9 0.2 collective-permute-done.3.refs_3_
  37.1 1.1 shard_map.80
  38.2 0.6 collective-permute-start.11
  38.8 1.7 %collective-permute-start.12 = (f32[10,8,512]{2,1,0:T(8,128)S(1)}, f32[10,8,512]{2,1,0:T(8,128)S(1)}, u32[]{:S(2)}, u32[]{:S(2)}) collective-permute-start(f32[10,8,512]{2,1,0:T(8,128)S(1)} %get-tuple-element.53), channel_id=1, source_target_pairs={{0,4},{2,6},{4,0},{6,2},{8,12},{10,14},{12,8},{14,10},{1,5},{3,7},... | collective-permute-start | bytes 491528 | tf_op jit(solution)/shard_map/ppermute | solution.py:318
  40.6 1.2 %collective-permute-start.13 = (f32[10,8,512]{2,1,0:T(8,128)S(1)}, f32[10,8,512]{2,1,0:T(8,128)S(1)}, u32[]{:S(2)}, u32[]{:S(2)}) collective-permute-start(f32[10,8,512]{2,1,0:T(8,128)S(1)} %get-tuple-element.54), channel_id=1, source_target_pairs={{0,6},{2,4},{4,2},{6,0},{8,14},{10,12},{12,10},{14,8},{1,7},{3,5},... | collective-permute-start | bytes 491528 | tf_op jit(solution)/shard_map/ppermute | solution.py:318
  41.8 1.3 %collective-permute-start.14 = (f32[10,8,512]{2,1,0:T(8,128)S(1)}, f32[10,8,512]{2,1,0:T(8,128)S(1)}, u32[]{:S(2)}, u32[]{:S(2)}) collective-permute-start(f32[10,8,512]{2,1,0:T(8,128)S(1)} %get-tuple-element.55), channel_id=1, source_target_pairs={{0,8},{2,10},{4,12},{6,14},{8,0},{10,2},{12,4},{14,6},{1,9},{3,11}... | collective-permute-start | bytes 491528 | tf_op jit(solution)/shard_map/ppermute | solution.py:318
  43.1 0.6 collective-permute-start.15
  43.8 1.6 %collective-permute-done.11.refs_1_.refs_5_ = f32[10,8,512]{2,1,0:T(8,128)S(1)} collective-permute-done((f32[10,8,512]{2,1,0:T(8,128)S(1)}, f32[10,8,512]{2,1,0:T(8,128)S(1)}, u32[]{:S(2)}, u32[]{:S(2)}) %collective-permute-start.11) | collective-permute-done | bytes 163872 | tf_op jit(solution)/shard_map/ppermute | solution.py:318
  45.4 1.9 %collective-permute-start.16 = (f32[10,8,512]{2,1,0:T(8,128)S(1)}, f32[10,8,512]{2,1,0:T(8,128)S(1)}, u32[]{:S(2)}, u32[]{:S(2)}) collective-permute-start(f32[10,8,512]{2,1,0:T(8,128)S(1)} %get-tuple-element.57), channel_id=1, source_target_pairs={{0,12},{2,14},{4,8},{6,10},{8,4},{10,6},{12,0},{14,2},{1,13},{3,15... | collective-permute-start | bytes 491528 | tf_op jit(solution)/shard_map/ppermute | solution.py:318
  47.3 3.1 %collective-permute-start.17 = (f32[10,8,512]{2,1,0:T(8,128)S(1)}, f32[10,8,512]{2,1,0:T(8,128)S(1)}, u32[]{:S(2)}, u32[]{:S(2)}) collective-permute-start(f32[10,8,512]{2,1,0:T(8,128)S(1)} %get-tuple-element.58), channel_id=1, source_target_pairs={{0,14},{2,12},{4,10},{6,8},{8,6},{10,4},{12,2},{14,0},{1,15},{3,13... | collective-permute-start | bytes 491528 | tf_op jit(solution)/shard_map/ppermute | solution.py:318
  50.4 4.8 %shard_map.82 = (bf16[10,512,512]{2,1,0:T(8,128)(2,1)S(1)}, bf16[10,512,512]{2,1,0:T(8,128)(2,1)S(1)}) custom-call(s32[10]{0:T(128)S(1)} %get-tuple-element.40.is_diag, f32[10,512,512]{2,1,0:T(8,128)} %tiles.3, f32[10,8,512]{2,1,0:T(8,128)S(1)} %get-tuple-element.47.after.refs_0_.refs_4_), custom_call_target="tpu_custom_call" | custom-call | bytes 20971520 | tf_op jit(solution)/shard_map/pallas_call | solution.py:337
  55.3 1.8 %collective-permute-done.16.refs_6_.refs_10_ = f32[10,8,512]{2,1,0:T(8,128)S(1)} collective-permute-done((f32[10,8,512]{2,1,0:T(8,128)S(1)}, f32[10,8,512]{2,1,0:T(8,128)S(1)}, u32[]{:S(2)}, u32[]{:S(2)}) %collective-permute-start.16) | collective-permute-done | bytes 163872 | tf_op jit(solution)/shard_map/ppermute | solution.py:318
  57.1 2.0 %collective-permute-done.17.refs_7_.refs_11_ = f32[10,8,512]{2,1,0:T(8,128)S(1)} collective-permute-done((f32[10,8,512]{2,1,0:T(8,128)S(1)}, f32[10,8,512]{2,1,0:T(8,128)S(1)}, u32[]{:S(2)}, u32[]{:S(2)}) %collective-permute-start.17) | collective-permute-done | bytes 163872 | tf_op jit(solution)/shard_map/ppermute | solution.py:318
  59.1 5.2 %shard_map.83 = (f32[2,16,4096]{2,1,0:T(8,128)S(1)}, f32[2,16,4096]{2,1,0:T(8,128)S(1)}) custom-call(s32[10]{0:T(128)S(1)} %get-tuple-element.39.row_local, s32[5]{0:T(128)S(1)} %stack.23.place, bf16[10,512,512]{2,1,0:T(8,128)(2,1)S(1)} %get-tuple-element.50.tile_hi, bf16[10,512,512]{2,1,0:T(8,128)(2,1)S(1)} %get-tuple-element.51.tile_lo, ...), custom_call_target="tpu_custom_call" | custom-call | tf_op jit(solution)/shard_map/pallas_call | solution.py:337
  64.3 0.1 collective-permute-start.18
  64.4 1.9 %collective-permute-done.18.refs_1_ = f32[2,16,4096]{2,1,0:T(8,128)S(1)} collective-permute-done((f32[2,16,4096]{2,1,0:T(8,128)S(1)}, f32[2,16,4096]{2,1,0:T(8,128)S(1)}, u32[]{:S(2)}, u32[]{:S(2)}) %collective-permute-start.18) | collective-permute-done | bytes 524320 | tf_op jit(solution)/shard_map/ppermute | solution.py:318
  66.3 1.5 %collective-permute-start.19 = (f32[16,4096]{1,0:T(8,128)S(1)}, f32[16,4096]{1,0:T(8,128)S(1)}, u32[]{:S(2)}, u32[]{:S(2)}) collective-permute-start(f32[16,4096]{1,0:T(8,128)S(1)} %fusion), channel_id=1, source_target_pairs={{0,2},{2,0},{1,3},{3,1},{4,6},{6,4},{5,7},{7,5},{8,10},{10,8},{9,1... | collective-permute-start | bytes 786440 | tf_op jit(solution)/shard_map/ppermute | solution.py:318
  67.8 6.9 %collective-permute-done.19.refs_4_ = f32[16,4096]{1,0:T(8,128)S(1)} collective-permute-done((f32[16,4096]{1,0:T(8,128)S(1)}, f32[16,4096]{1,0:T(8,128)S(1)}, u32[]{:S(2)}, u32[]{:S(2)}) %collective-permute-start.19) | collective-permute-done | bytes 262176 | tf_op jit(solution)/shard_map/ppermute | solution.py:318
  74.7 0.1 shard_map.84
  74.8 1.5 %collective-permute-start.28 = (f32[16,4096]{1,0:T(8,128)S(1)}, f32[16,4096]{1,0:T(8,128)S(1)}, u32[]{:S(2)}, u32[]{:S(2)}) collective-permute-start(f32[16,4096]{1,0:T(8,128)S(1)} %get-tuple-element.63.refs_8_.refs_0_), channel_id=1, source_target_pairs={{0,2},{2,0},{1,3},{3,1},{4,6},{6,4},{5,7},{7,5},{8,10},{10,8},{9,1... | collective-permute-start | bytes 786440 | tf_op jit(solution)/shard_map/ppermute | solution.py:318
  76.3 1.5 %collective-permute-start.24 = (f32[8,4096]{1,0:T(8,128)S(1)}, f32[8,4096]{1,0:T(8,128)S(1)}, u32[]{:S(2)}, u32[]{:S(2)}) collective-permute-start(f32[8,4096]{1,0:T(8,128)S(1)} %get-tuple-element.61), channel_id=1, source_target_pairs={{0,16},{1,20},{4,17},{5,21},{8,24},{9,28},{12,25},{13,29},{16,0},{... | collective-permute-start | bytes 393224 | tf_op jit(solution)/shard_map/ppermute | solution.py:318
  77.9 0.7 collective-permute-start.20
  78.5 2.0 %collective-permute-start.26 = (f32[8,4096]{1,0:T(8,128)S(1)}, f32[8,4096]{1,0:T(8,128)S(1)}, u32[]{:S(2)}, u32[]{:S(2)}) collective-permute-start(f32[8,4096]{1,0:T(8,128)S(1)} %get-tuple-element.62), channel_id=1, source_target_pairs={{0,24},{1,28},{4,25},{5,29},{8,16},{9,20},{12,17},{13,21},{16,8},{... | collective-permute-start | bytes 393224 | tf_op jit(solution)/shard_map/ppermute | solution.py:318
  80.5 8.6 %collective-permute-done.24.refs_4_ = f32[8,4096]{1,0:T(8,128)S(1)} collective-permute-done((f32[8,4096]{1,0:T(8,128)S(1)}, f32[8,4096]{1,0:T(8,128)S(1)}, u32[]{:S(2)}, u32[]{:S(2)}) %collective-permute-start.24) | collective-permute-done | bytes 131104 | tf_op jit(solution)/shard_map/ppermute | solution.py:318
  89.2 0.5 collective-permute-start.25
  89.7 0.1 collective-permute-start.21
  89.8 4.4 %collective-permute-done.22.refs_2_ = f32[8,4096]{1,0:T(8,128)S(1)} collective-permute-done((f32[8,4096]{1,0:T(8,128)S(1)}, f32[8,4096]{1,0:T(8,128)S(1)}, u32[]{:S(2)}, u32[]{:S(2)}) %collective-permute-start.22) | collective-permute-done | bytes 131104 | tf_op jit(solution)/shard_map/ppermute | solution.py:318
  94.1 0.5 collective-permute-start.23
  94.6 0.8 collective-permute-done.27.refs_7_
  95.5 0.2 collective-permute-done.23.refs_3_
  95.7 1.1 shard_map.85
  96.8 0.6 collective-permute-start.31
  97.4 2.9 %collective-permute-start.33 = (f32[10,8,512]{2,1,0:T(8,128)S(1)}, f32[10,8,512]{2,1,0:T(8,128)S(1)}, u32[]{:S(2)}, u32[]{:S(2)}) collective-permute-start(f32[10,8,512]{2,1,0:T(8,128)S(1)} %get-tuple-element.68), channel_id=1, source_target_pairs={{0,6},{2,4},{4,2},{6,0},{8,14},{10,12},{12,10},{14,8},{1,7},{3,5},... | collective-permute-start | bytes 491528 | tf_op jit(solution)/shard_map/ppermute | solution.py:318
  100.3 0.0 collective-permute-start.34
  100.3 2.0 %collective-permute-start.35 = (f32[10,8,512]{2,1,0:T(8,128)S(1)}, f32[10,8,512]{2,1,0:T(8,128)S(1)}, u32[]{:S(2)}, u32[]{:S(2)}) collective-permute-start(f32[10,8,512]{2,1,0:T(8,128)S(1)} %get-tuple-element.70), channel_id=1, source_target_pairs={{0,10},{2,8},{4,14},{6,12},{8,2},{10,0},{12,6},{14,4},{1,11},{3,9}... | collective-permute-start | bytes 491528 | tf_op jit(solution)/shard_map/ppermute | solution.py:318
  102.4 1.6 %collective-permute-done.31.refs_1_ = f32[10,8,512]{2,1,0:T(8,128)S(1)} collective-permute-done((f32[10,8,512]{2,1,0:T(8,128)S(1)}, f32[10,8,512]{2,1,0:T(8,128)S(1)}, u32[]{:S(2)}, u32[]{:S(2)}) %collective-permute-start.31) | collective-permute-done | bytes 163872 | tf_op jit(solution)/shard_map/ppermute | solution.py:318
  103.9 3.1 %collective-permute-done.32.refs_2_ = f32[10,8,512]{2,1,0:T(8,128)S(1)} collective-permute-done((f32[10,8,512]{2,1,0:T(8,128)S(1)}, f32[10,8,512]{2,1,0:T(8,128)S(1)}, u32[]{:S(2)}, u32[]{:S(2)}) %collective-permute-start.32) | collective-permute-done | bytes 163872 | tf_op jit(solution)/shard_map/ppermute | solution.py:318
  107.1 1.5 %shard_map.81 = (f32[64,4096]{1,0:T(8,128)S(1)}, bf16[8,512,192]{2,1,0:T(8,128)(2,1)S(1)}) custom-call(s32[5]{0:T(128)S(1)} %stack.23.place, f32[10,8,512]{2,1,0:T(8,128)S(1)} %get-tuple-element.47.after.refs_0_.refs_4_, f32[16,4096]{1,0:T(8,128)S(1)} %get-tuple-element.46.refs_8_.refs_0_.refs_2_, f32[16,4096]{1,0:T(8,128)S(1)} %collective-permute-done.8.refs_9_.refs_1_, ...), custom_call_target="tpu_custom_call" | custom-call | bytes 4194304 | tf_op jit(solution)/shard_map/pallas_call | solution.py:337
  108.6 6.3 %shard_map.86 = (f32[10,512,512]{2,1,0:T(8,128)S(1)}, f32[1,4096]{1,0:T(1,128)}) custom-call(s32[10]{0:T(128)S(1)} %get-tuple-element.39.row_local, s32[5]{0:T(128)S(1)} %stack.23.place, f32[10,512,512]{2,1,0:T(8,128)} %tiles.3, f32[1,4096]{1,0:T(1,128)S(1)} %bitcast.10, f32[64,4096]{1,0:T(8,128)S(1)} %get-tuple-element.49.resid_rows, ...), custom_call_target="tpu_custom_call" | custom-call | flops 1006632960 | bytes 41943040 | tf_op jit(solution)/shard_map/pallas_call | solution.py:337
  114.9 1.3 %collective-permute-done.37.refs_7_ = f32[10,8,512]{2,1,0:T(8,128)S(1)} collective-permute-done((f32[10,8,512]{2,1,0:T(8,128)S(1)}, f32[10,8,512]{2,1,0:T(8,128)S(1)}, u32[]{:S(2)}, u32[]{:S(2)}) %collective-permute-start.37) | collective-permute-done | bytes 163872 | tf_op jit(solution)/shard_map/ppermute | solution.py:318
  116.2 4.8 %shard_map.87 = f32[10,512,512]{2,1,0:T(8,128)} custom-call(s32[10]{0:T(128)S(1)} %get-tuple-element.39.row_local, s32[10]{0:T(128)S(1)} %get-tuple-element.40.is_diag, bf16[8,512,192]{2,1,0:T(8,128)(2,1)S(1)} %get-tuple-element.48.left, f32[10,512,512]{2,1,0:T(8,128)S(1)} %get-tuple-element.65.partial, f32[10,8,512]{2,1,0:T(8,128)S(1)} %get-tuple-element.64.after.refs_0_, ...), custom_call_target="tpu_custom_call" | custom-call | tf_op jit(solution)/shard_map/pallas_call | solution.py:337
  (33 shorter events, 0.1 us)
Async XLA Ops:
  4.0 14.7 %all-to-all-start = ((f32[8,16,256]{2,1,0:T(8,128)}), f32[8,16,256]{2,1,0:T(8,128)S(1)}, u32[]{:S(2)}, u32[]{:S(2)}) async-start(f32[8,16,256]{2,1,0:T(8,128)} %get-tuple-element.38.after), calls=%async_computation | async-start | bytes 262144 | tf_op jit(solution)/shard_map/all_to_all | solution.py:370
  11.4 0.7 copy-start.1
  12.1 0.7 copy-start.2
  19.6 14.4 %collective-permute-start.8 = (f32[16,4096]{1,0:T(8,128)S(1)}, f32[16,4096]{1,0:T(8,128)S(1)}, u32[]{:S(2)}, u32[]{:S(2)}) collective-permute-start(f32[16,4096]{1,0:T(8,128)S(1)} %get-tuple-element.46.refs_8_.refs_0_.refs_2_), channel_id=1, source_target_pairs={{0,2},{2,0},{1,3},{3,1},{4,6},{6,4},{5,7},{7,5},{8,10},{10,8},{9,1... | collective-permute-start | bytes 786440 | tf_op jit(solution)/shard_map/ppermute | solution.py:318
  21.2 12.3 %collective-permute-start.4 = (f32[8,4096]{1,0:T(8,128)S(1)}, f32[8,4096]{1,0:T(8,128)S(1)}, u32[]{:S(2)}, u32[]{:S(2)}) collective-permute-start(f32[8,4096]{1,0:T(8,128)S(1)} %get-tuple-element.44), channel_id=1, source_target_pairs={{0,16},{1,20},{4,17},{5,21},{8,24},{9,28},{12,25},{13,29},{16,0},{... | collective-permute-start | bytes 393224 | tf_op jit(solution)/shard_map/ppermute | solution.py:318
  21.6 11.9 %collective-permute-start = (f32[8,4096]{1,0:T(8,128)S(1)}, f32[8,4096]{1,0:T(8,128)S(1)}, u32[]{:S(2)}, u32[]{:S(2)}) collective-permute-start(f32[8,4096]{1,0:T(8,128)S(1)} %get-tuple-element.44), channel_id=1, source_target_pairs={{0,0},{1,4},{4,1},{5,5},{8,8},{9,12},{12,9},{13,13},{16,16},{17,20... | collective-permute-start | bytes 393224 | tf_op jit(solution)/shard_map/ppermute | solution.py:318
  22.3 11.9 %collective-permute-start.6 = (f32[8,4096]{1,0:T(8,128)S(1)}, f32[8,4096]{1,0:T(8,128)S(1)}, u32[]{:S(2)}, u32[]{:S(2)}) collective-permute-start(f32[8,4096]{1,0:T(8,128)S(1)} %get-tuple-element.45), channel_id=1, source_target_pairs={{0,24},{1,28},{4,25},{5,29},{8,16},{9,20},{12,17},{13,21},{16,8},{... | collective-permute-start | bytes 393224 | tf_op jit(solution)/shard_map/ppermute | solution.py:318
  24.2 11.4 %collective-permute-start.2 = (f32[8,4096]{1,0:T(8,128)S(1)}, f32[8,4096]{1,0:T(8,128)S(1)}, u32[]{:S(2)}, u32[]{:S(2)}) collective-permute-start(f32[8,4096]{1,0:T(8,128)S(1)} %get-tuple-element.45), channel_id=1, source_target_pairs={{0,8},{1,12},{4,9},{5,13},{8,0},{9,4},{12,1},{13,5},{16,24},{17,28... | collective-permute-start | bytes 393224 | tf_op jit(solution)/shard_map/ppermute | solution.py:318
  33.5 2.0 %collective-permute-start.5 = (f32[8,4096]{1,0:T(8,128)S(1)}, f32[8,4096]{1,0:T(8,128)S(1)}, u32[]{:S(2)}, u32[]{:S(2)}) collective-permute-start(f32[8,4096]{1,0:T(8,128)S(1)} %collective-permute-done.4.refs_4_), channel_id=1, source_target_pairs={{0,1},{1,0},{2,3},{3,2},{4,5},{5,4},{6,7},{7,6},{8,9},{9,8},{10,11... | collective-permute-start | bytes 393224 | tf_op jit(solution)/shard_map/ppermute | solution.py:318
  33.5 3.6 %collective-permute-start.9 = (f32[16,4096]{1,0:T(8,128)S(1)}, f32[16,4096]{1,0:T(8,128)S(1)}, u32[]{:S(2)}, u32[]{:S(2)}) collective-permute-start(f32[16,4096]{1,0:T(8,128)S(1)} %get-tuple-element.46.refs_8_.refs_0_.refs_2_), channel_id=1, source_target_pairs={{0,1},{1,0},{2,3},{3,2},{4,5},{5,4},{6,7},{7,6},{8,9},{9,8},{10,11... | collective-permute-start | bytes 786440 | tf_op jit(solution)/shard_map/ppermute | solution.py:318
  34.1 3.1 %collective-permute-start.10 = (f32[16,4096]{1,0:T(8,128)S(1)}, f32[16,4096]{1,0:T(8,128)S(1)}, u32[]{:S(2)}, u32[]{:S(2)}) collective-permute-start(f32[16,4096]{1,0:T(8,128)S(1)} %collective-permute-done.8.refs_9_.refs_1_), channel_id=1, source_target_pairs={{0,1},{1,0},{2,3},{3,2},{4,5},{5,4},{6,7},{7,6},{8,9},{9,8},{10,11... | collective-permute-start | bytes 786440 | tf_op jit(solution)/shard_map/ppermute | solution.py:318
  34.1 2.0 %collective-permute-start.1 = (f32[8,4096]{1,0:T(8,128)S(1)}, f32[8,4096]{1,0:T(8,128)S(1)}, u32[]{:S(2)}, u32[]{:S(2)}) collective-permute-start(f32[8,4096]{1,0:T(8,128)S(1)} %collective-permute-done.refs_0_), channel_id=1, source_target_pairs={{0,1},{1,0},{2,3},{3,2},{4,5},{5,4},{6,7},{7,6},{8,9},{9,8},{10,11... | collective-permute-start | bytes 393224 | tf_op jit(solution)/shard_map/ppermute | solution.py:318
  35.6 1.3 %collective-permute-start.7 = (f32[8,4096]{1,0:T(8,128)S(1)}, f32[8,4096]{1,0:T(8,128)S(1)}, u32[]{:S(2)}, u32[]{:S(2)}) collective-permute-start(f32[8,4096]{1,0:T(8,128)S(1)} %collective-permute-done.6.refs_6_), channel_id=1, source_target_pairs={{0,1},{1,0},{2,3},{3,2},{4,5},{5,4},{6,7},{7,6},{8,9},{9,8},{10,11... | collective-permute-start | bytes 393224 | tf_op jit(solution)/shard_map/ppermute | solution.py:318
  35.6 1.5 %collective-permute-start.3 = (f32[8,4096]{1,0:T(8,128)S(1)}, f32[8,4096]{1,0:T(8,128)S(1)}, u32[]{:S(2)}, u32[]{:S(2)}) collective-permute-start(f32[8,4096]{1,0:T(8,128)S(1)} %collective-permute-done.2.refs_2_), channel_id=1, source_target_pairs={{0,1},{1,0},{2,3},{3,2},{4,5},{5,4},{6,7},{7,6},{8,9},{9,8},{10,11... | collective-permute-start | bytes 393224 | tf_op jit(solution)/shard_map/ppermute | solution.py:318
  38.2 7.1 %collective-permute-start.11 = (f32[10,8,512]{2,1,0:T(8,128)S(1)}, f32[10,8,512]{2,1,0:T(8,128)S(1)}, u32[]{:S(2)}, u32[]{:S(2)}) collective-permute-start(f32[10,8,512]{2,1,0:T(8,128)S(1)} %get-tuple-element.52), channel_id=1, source_target_pairs={{0,2},{2,0},{4,6},{6,4},{8,10},{10,8},{12,14},{14,12},{1,3},{3,1},... | collective-permute-start | bytes 491528 | tf_op jit(solution)/shard_map/ppermute | solution.py:318
  38.8 8.5 %collective-permute-start.12 = (f32[10,8,512]{2,1,0:T(8,128)S(1)}, f32[10,8,512]{2,1,0:T(8,128)S(1)}, u32[]{:S(2)}, u32[]{:S(2)}) collective-permute-start(f32[10,8,512]{2,1,0:T(8,128)S(1)} %get-tuple-element.53), channel_id=1, source_target_pairs={{0,4},{2,6},{4,0},{6,2},{8,12},{10,14},{12,8},{14,10},{1,5},{3,7},... | collective-permute-start | bytes 491528 | tf_op jit(solution)/shard_map/ppermute | solution.py:318
  40.6 14.7 %collective-permute-start.13 = (f32[10,8,512]{2,1,0:T(8,128)S(1)}, f32[10,8,512]{2,1,0:T(8,128)S(1)}, u32[]{:S(2)}, u32[]{:S(2)}) collective-permute-start(f32[10,8,512]{2,1,0:T(8,128)S(1)} %get-tuple-element.54), channel_id=1, source_target_pairs={{0,6},{2,4},{4,2},{6,0},{8,14},{10,12},{12,10},{14,8},{1,7},{3,5},... | collective-permute-start | bytes 491528 | tf_op jit(solution)/shard_map/ppermute | solution.py:318
  41.8 13.5 %collective-permute-start.14 = (f32[10,8,512]{2,1,0:T(8,128)S(1)}, f32[10,8,512]{2,1,0:T(8,128)S(1)}, u32[]{:S(2)}, u32[]{:S(2)}) collective-permute-start(f32[10,8,512]{2,1,0:T(8,128)S(1)} %get-tuple-element.55), channel_id=1, source_target_pairs={{0,8},{2,10},{4,12},{6,14},{8,0},{10,2},{12,4},{14,6},{1,9},{3,11}... | collective-permute-start | bytes 491528 | tf_op jit(solution)/shard_map/ppermute | solution.py:318
  43.1 12.1 %collective-permute-start.15 = (f32[10,8,512]{2,1,0:T(8,128)S(1)}, f32[10,8,512]{2,1,0:T(8,128)S(1)}, u32[]{:S(2)}, u32[]{:S(2)}) collective-permute-start(f32[10,8,512]{2,1,0:T(8,128)S(1)} %get-tuple-element.56), channel_id=1, source_target_pairs={{0,10},{2,8},{4,14},{6,12},{8,2},{10,0},{12,6},{14,4},{1,11},{3,9}... | collective-permute-start | bytes 491528 | tf_op jit(solution)/shard_map/ppermute | solution.py:318
  45.4 11.7 %collective-permute-start.16 = (f32[10,8,512]{2,1,0:T(8,128)S(1)}, f32[10,8,512]{2,1,0:T(8,128)S(1)}, u32[]{:S(2)}, u32[]{:S(2)}) collective-permute-start(f32[10,8,512]{2,1,0:T(8,128)S(1)} %get-tuple-element.57), channel_id=1, source_target_pairs={{0,12},{2,14},{4,8},{6,10},{8,4},{10,6},{12,0},{14,2},{1,13},{3,15... | collective-permute-start | bytes 491528 | tf_op jit(solution)/shard_map/ppermute | solution.py:318
  47.3 11.8 %collective-permute-start.17 = (f32[10,8,512]{2,1,0:T(8,128)S(1)}, f32[10,8,512]{2,1,0:T(8,128)S(1)}, u32[]{:S(2)}, u32[]{:S(2)}) collective-permute-start(f32[10,8,512]{2,1,0:T(8,128)S(1)} %get-tuple-element.58), channel_id=1, source_target_pairs={{0,14},{2,12},{4,10},{6,8},{8,6},{10,4},{12,2},{14,0},{1,15},{3,13... | collective-permute-start | bytes 491528 | tf_op jit(solution)/shard_map/ppermute | solution.py:318
  59.1 15.7 %copy-start = (f32[4096]{0:T(1024)S(1)}, f32[4096]{0:T(1024)}, u32[]{:S(2)}) copy-start(f32[4096]{0:T(1024)} %param.9) | copy-start | bytes 49156
  64.3 2.0 %collective-permute-start.18 = (f32[2,16,4096]{2,1,0:T(8,128)S(1)}, f32[2,16,4096]{2,1,0:T(8,128)S(1)}, u32[]{:S(2)}, u32[]{:S(2)}) collective-permute-start(f32[2,16,4096]{2,1,0:T(8,128)S(1)} %get-tuple-element.60), channel_id=1, source_target_pairs={{0,1},{1,0},{2,3},{3,2},{4,5},{5,4},{6,7},{7,6},{8,9},{9,8},{10,11... | collective-permute-start | bytes 1572872 | tf_op jit(solution)/shard_map/ppermute | solution.py:318
  66.3 8.4 %collective-permute-start.19 = (f32[16,4096]{1,0:T(8,128)S(1)}, f32[16,4096]{1,0:T(8,128)S(1)}, u32[]{:S(2)}, u32[]{:S(2)}) collective-permute-start(f32[16,4096]{1,0:T(8,128)S(1)} %fusion), channel_id=1, source_target_pairs={{0,2},{2,0},{1,3},{3,1},{4,6},{6,4},{5,7},{7,5},{8,10},{10,8},{9,1... | collective-permute-start | bytes 786440 | tf_op jit(solution)/shard_map/ppermute | solution.py:318
  74.8 14.3 %collective-permute-start.28 = (f32[16,4096]{1,0:T(8,128)S(1)}, f32[16,4096]{1,0:T(8,128)S(1)}, u32[]{:S(2)}, u32[]{:S(2)}) collective-permute-start(f32[16,4096]{1,0:T(8,128)S(1)} %get-tuple-element.63.refs_8_.refs_0_), channel_id=1, source_target_pairs={{0,2},{2,0},{1,3},{3,1},{4,6},{6,4},{5,7},{7,5},{8,10},{10,8},{9,1... | collective-permute-start | bytes 786440 | tf_op jit(solution)/shard_map/ppermute | solution.py:318
  76.3 12.8 %collective-permute-start.24 = (f32[8,4096]{1,0:T(8,128)S(1)}, f32[8,4096]{1,0:T(8,128)S(1)}, u32[]{:S(2)}, u32[]{:S(2)}) collective-permute-start(f32[8,4096]{1,0:T(8,128)S(1)} %get-tuple-element.61), channel_id=1, source_target_pairs={{0,16},{1,20},{4,17},{5,21},{8,24},{9,28},{12,25},{13,29},{16,0},{... | collective-permute-start | bytes 393224 | tf_op jit(solution)/shard_map/ppermute | solution.py:318
  77.9 16.2 %collective-permute-start.29 = (f32[16,4096]{1,0:T(8,128)S(1)}, f32[16,4096]{1,0:T(8,128)S(1)}, u32[]{:S(2)}, u32[]{:S(2)}) collective-permute-start(f32[16,4096]{1,0:T(8,128)S(1)} %get-tuple-element.63.refs_8_.refs_0_), channel_id=1, source_target_pairs={{0,1},{1,0},{2,3},{3,2},{4,5},{5,4},{6,7},{7,6},{8,9},{9,8},{10,11... | collective-permute-start | bytes 786440 | tf_op jit(solution)/shard_map/ppermute | solution.py:318
  77.9 11.3 %collective-permute-start.20 = (f32[8,4096]{1,0:T(8,128)S(1)}, f32[8,4096]{1,0:T(8,128)S(1)}, u32[]{:S(2)}, u32[]{:S(2)}) collective-permute-start(f32[8,4096]{1,0:T(8,128)S(1)} %get-tuple-element.61), channel_id=1, source_target_pairs={{0,0},{1,4},{4,1},{5,5},{8,8},{9,12},{12,9},{13,13},{16,16},{17,20... | collective-permute-start | bytes 393224 | tf_op jit(solution)/shard_map/ppermute | solution.py:318
  78.5 11.1 %collective-permute-start.26 = (f32[8,4096]{1,0:T(8,128)S(1)}, f32[8,4096]{1,0:T(8,128)S(1)}, u32[]{:S(2)}, u32[]{:S(2)}) collective-permute-start(f32[8,4096]{1,0:T(8,128)S(1)} %get-tuple-element.62), channel_id=1, source_target_pairs={{0,24},{1,28},{4,25},{5,29},{8,16},{9,20},{12,17},{13,21},{16,8},{... | collective-permute-start | bytes 393224 | tf_op jit(solution)/shard_map/ppermute | solution.py:318
  89.1 5.0 %collective-permute-start.22 = (f32[8,4096]{1,0:T(8,128)S(1)}, f32[8,4096]{1,0:T(8,128)S(1)}, u32[]{:S(2)}, u32[]{:S(2)}) collective-permute-start(f32[8,4096]{1,0:T(8,128)S(1)} %get-tuple-element.62), channel_id=1, source_target_pairs={{0,8},{1,12},{4,9},{5,13},{8,0},{9,4},{12,1},{13,5},{16,24},{17,28... | collective-permute-start | bytes 393224 | tf_op jit(solution)/shard_map/ppermute | solution.py:318
  89.2 6.5 %collective-permute-start.30 = (f32[16,4096]{1,0:T(8,128)S(1)}, f32[16,4096]{1,0:T(8,128)S(1)}, u32[]{:S(2)}, u32[]{:S(2)}) collective-permute-start(f32[16,4096]{1,0:T(8,128)S(1)} %collective-permute-done.28.refs_9_.refs_1_), channel_id=1, source_target_pairs={{0,1},{1,0},{2,3},{3,2},{4,5},{5,4},{6,7},{7,6},{8,9},{9,8},{10,11... | collective-permute-start | bytes 786440 | tf_op jit(solution)/shard_map/ppermute | solution.py:318
  89.2 5.5 %collective-permute-start.25 = (f32[8,4096]{1,0:T(8,128)S(1)}, f32[8,4096]{1,0:T(8,128)S(1)}, u32[]{:S(2)}, u32[]{:S(2)}) collective-permute-start(f32[8,4096]{1,0:T(8,128)S(1)} %collective-permute-done.24.refs_4_), channel_id=1, source_target_pairs={{0,1},{1,0},{2,3},{3,2},{4,5},{5,4},{6,7},{7,6},{8,9},{9,8},{10,11... | collective-permute-start | bytes 393224 | tf_op jit(solution)/shard_map/ppermute | solution.py:318
  89.7 5.0 %collective-permute-start.21 = (f32[8,4096]{1,0:T(8,128)S(1)}, f32[8,4096]{1,0:T(8,128)S(1)}, u32[]{:S(2)}, u32[]{:S(2)}) collective-permute-start(f32[8,4096]{1,0:T(8,128)S(1)} %collective-permute-done.20.refs_0_), channel_id=1, source_target_pairs={{0,1},{1,0},{2,3},{3,2},{4,5},{5,4},{6,7},{7,6},{8,9},{9,8},{10,11... | collective-permute-start | bytes 393224 | tf_op jit(solution)/shard_map/ppermute | solution.py:318
  94.1 1.3 %collective-permute-start.27 = (f32[8,4096]{1,0:T(8,128)S(1)}, f32[8,4096]{1,0:T(8,128)S(1)}, u32[]{:S(2)}, u32[]{:S(2)}) collective-permute-start(f32[8,4096]{1,0:T(8,128)S(1)} %collective-permute-done.26.refs_6_), channel_id=1, source_target_pairs={{0,1},{1,0},{2,3},{3,2},{4,5},{5,4},{6,7},{7,6},{8,9},{9,8},{10,11... | collective-permute-start | bytes 393224 | tf_op jit(solution)/shard_map/ppermute | solution.py:318
  94.1 1.5 %collective-permute-start.23 = (f32[8,4096]{1,0:T(8,128)S(1)}, f32[8,4096]{1,0:T(8,128)S(1)}, u32[]{:S(2)}, u32[]{:S(2)}) collective-permute-start(f32[8,4096]{1,0:T(8,128)S(1)} %collective-permute-done.22.refs_2_), channel_id=1, source_target_pairs={{0,1},{1,0},{2,3},{3,2},{4,5},{5,4},{6,7},{7,6},{8,9},{9,8},{10,11... | collective-permute-start | bytes 393224 | tf_op jit(solution)/shard_map/ppermute | solution.py:318
  96.8 7.1 %collective-permute-start.31 = (f32[10,8,512]{2,1,0:T(8,128)S(1)}, f32[10,8,512]{2,1,0:T(8,128)S(1)}, u32[]{:S(2)}, u32[]{:S(2)}) collective-permute-start(f32[10,8,512]{2,1,0:T(8,128)S(1)} %get-tuple-element.66), channel_id=1, source_target_pairs={{0,2},{2,0},{4,6},{6,4},{8,10},{10,8},{12,14},{14,12},{1,3},{3,1},... | collective-permute-start | bytes 491528 | tf_op jit(solution)/shard_map/ppermute | solution.py:318
  97.4 9.7 %collective-permute-start.32 = (f32[10,8,512]{2,1,0:T(8,128)S(1)}, f32[10,8,512]{2,1,0:T(8,128)S(1)}, u32[]{:S(2)}, u32[]{:S(2)}) collective-permute-start(f32[10,8,512]{2,1,0:T(8,128)S(1)} %get-tuple-element.67), channel_id=1, source_target_pairs={{0,4},{2,6},{4,0},{6,2},{8,12},{10,14},{12,8},{14,10},{1,5},{3,7},... | collective-permute-start | bytes 491528 | tf_op jit(solution)/shard_map/ppermute | solution.py:318
  97.4 17.5 %collective-permute-start.33 = (f32[10,8,512]{2,1,0:T(8,128)S(1)}, f32[10,8,512]{2,1,0:T(8,128)S(1)}, u32[]{:S(2)}, u32[]{:S(2)}) collective-permute-start(f32[10,8,512]{2,1,0:T(8,128)S(1)} %get-tuple-element.68), channel_id=1, source_target_pairs={{0,6},{2,4},{4,2},{6,0},{8,14},{10,12},{12,10},{14,8},{1,7},{3,5},... | collective-permute-start | bytes 491528 | tf_op jit(solution)/shard_map/ppermute | solution.py:318
  100.3 14.6 %collective-permute-start.34 = (f32[10,8,512]{2,1,0:T(8,128)S(1)}, f32[10,8,512]{2,1,0:T(8,128)S(1)}, u32[]{:S(2)}, u32[]{:S(2)}) collective-permute-start(f32[10,8,512]{2,1,0:T(8,128)S(1)} %get-tuple-element.69), channel_id=1, source_target_pairs={{0,8},{2,10},{4,12},{6,14},{8,0},{10,2},{12,4},{14,6},{1,9},{3,11}... | collective-permute-start | bytes 491528 | tf_op jit(solution)/shard_map/ppermute | solution.py:318
  100.3 14.6 %collective-permute-start.35 = (f32[10,8,512]{2,1,0:T(8,128)S(1)}, f32[10,8,512]{2,1,0:T(8,128)S(1)}, u32[]{:S(2)}, u32[]{:S(2)}) collective-permute-start(f32[10,8,512]{2,1,0:T(8,128)S(1)} %get-tuple-element.70), channel_id=1, source_target_pairs={{0,10},{2,8},{4,14},{6,12},{8,2},{10,0},{12,6},{14,4},{1,11},{3,9}... | collective-permute-start | bytes 491528 | tf_op jit(solution)/shard_map/ppermute | solution.py:318
  103.9 11.0 %collective-permute-start.36 = (f32[10,8,512]{2,1,0:T(8,128)S(1)}, f32[10,8,512]{2,1,0:T(8,128)S(1)}, u32[]{:S(2)}, u32[]{:S(2)}) collective-permute-start(f32[10,8,512]{2,1,0:T(8,128)S(1)} %get-tuple-element.71), channel_id=1, source_target_pairs={{0,12},{2,14},{4,8},{6,10},{8,4},{10,6},{12,0},{14,2},{1,13},{3,15... | collective-permute-start | bytes 491528 | tf_op jit(solution)/shard_map/ppermute | solution.py:318
  107.1 9.1 %collective-permute-start.37 = (f32[10,8,512]{2,1,0:T(8,128)S(1)}, f32[10,8,512]{2,1,0:T(8,128)S(1)}, u32[]{:S(2)}, u32[]{:S(2)}) collective-permute-start(f32[10,8,512]{2,1,0:T(8,128)S(1)} %get-tuple-element.72), channel_id=1, source_target_pairs={{0,14},{2,12},{4,10},{6,8},{8,6},{10,4},{12,2},{14,0},{1,15},{3,13... | collective-permute-start | bytes 491528 | tf_op jit(solution)/shard_map/ppermute | solution.py:318
where the time goes:
time: 121 us
  waiting for transfers between devices  47.1 us (39%)
  starting transfers between devices  39.2 us (32%)
  Pallas kernels  32.5 us (27%)
  local copies, waits for them, and re-layouts  1.45 us (1%)
    ppermute x38, waiting for transfers between devices, permute(): lax.ppermute(value, names, [(at, flat(target(*coords_of(at)))) for at in...  44.3 us
    pallas_call x11, Pallas kernels, call(): pl.pallas_call(kernel, out_shape=[out for out, _ in outs], in_specs=specs...  32.5 us
    ppermute x38, starting transfers between devices, permute(): lax.ppermute(value, names, [(at, flat(target(*coords_of(at)))) for at in...  31.8 us
    all_to_all x1, starting transfers between devices, per_device(): score_terms = lax.all_to_all(score_copies, ROWS, 0, 0, tiled=True)  7.32 us
    all_to_all x1, waiting for transfers between devices, per_device(): score_terms = lax.all_to_all(score_copies, ROWS, 0, 0, tiled=True)  2.73 us
  transfers between devices with their start and end apart: 39, of which 17 were waited for; matrix products, arithmetic and copies ran while one was open for 0% of the time, Pallas kernels for 13%

commit v1 on v0

--- a/solution.py
+++ b/solution.py
@@ -14,10 +14,6 @@
 ROWS = ("a", "u", "v")
 COLS = ("x", "k")
 PLANE = ("u", "v", "x")
-
-
-def exchange_order(a_count):
-    return [(da, dz) for da in reversed(range(a_count)) for dz in (1, 0)]
 
 
 def plane_order(x_count):
@@ -165,7 +161,7 @@
 
 
 def product_kernel(x_count, row_local, place, tile_hi, tile_lo, *refs):
-    routed, (keep, give, total) = refs[:-3], refs[-3:]
+    routed, sides, total = refs[:-5], refs[-5:-1], refs[-1]
     blocks, samples, block = total.shape
     total[...] = jnp.zeros_like(total)
 
@@ -177,30 +173,31 @@
         return carry
 
     lax.fori_loop(0, tile_hi.shape[0], multiply, 0)
-    half = keep.shape[1] // 2
-    for out, core in ((keep, place[4]), (give, 1 - place[4])):
+    for side, out in enumerate(sides):
+        du, core = side // 2, place[4] ^ (side % 2)
+        half = out.shape[1]
         for dx in range(x_count):
-            for du in range(2):
-                source = (du * 2 + (place[2] ^ core)) * x_count + (x_count - dx) % x_count
-                start = pl.multiple_of(source * half, half)
-                for at in range(blocks):
-                    out[dx, du * half : (du + 1) * half, at * block : (at + 1) * block] = total[
-                        at, pl.ds(start, half), :
-                    ]
-
-
-def applied_kernel(count, *refs):
+            source = (du * 2 + (place[2] ^ core)) * x_count + (x_count - dx) % x_count
+            start = pl.multiple_of(source * half, half)
+            for at in range(blocks):
+                out[dx, :, at * block : (at + 1) * block] = total[at, pl.ds(start, half), :]
+
+
+def applied_kernel(du, count, *refs):
     keep, got, residual, diagonal = refs[:4]
     arrived = refs[4 : 4 + count]
-    whole, first, second = refs[4 + count :]
-    half = first.shape[0]
+    half = keep.shape[1]
     value = keep[0] + got[0]
     for other in arrived:
         value = value + other[...]
-    value = value + diagonal[...] * residual[...]
-    whole[...] = value
-    first[...] = value[:half]
-    second[...] = value[half:]
+    value = value + diagonal[...] * residual[du * half : (du + 1) * half]
+    if du == 0:
+        refs[-1][...] = value
+    else:
+        earlier, part, whole = refs[-3:]
+        part[...] = value
+        whole[:half] = earlier[...]
+        whole[half:] = value
 
 
 def place_rows(x_count, place, parts, rows):
@@ -394,25 +391,24 @@
             parts.append(shift_x(whole, dx))
         return parts + [swap_core(part) for part in parts]
 
-    def route(near, far, whole):
-        held = [None] * (2 * a_count)
-        for da, dz in exchange_order(a_count):
-            held[da * 2 + dz] = permute(
-                far if dz else near,
+    def exchange(part, dz):
+        held = [None] * a_count
+        for da in reversed(range(a_count)):
+            held[da] = permute(
+                part,
                 ("a", "u", "v", "k"),
                 lambda a, u, v, k: ((a + da) % a_count, u ^ dz, k, v),
             )
-        beside = own_rows(whole)
-        sources = []
-        for part in held:
-            sources += [part, swap_core(part)]
-        slots = call(
+        return [[arrived, swap_core(arrived)] for arrived in held]
+
+    def gather_slots(near, far, beside):
+        sources = [part for pair in zip(near, far) for parts in pair for part in parts]
+        return call(
             functools.partial(gather_kernel, len(sources), plane),
             [chip((tile_dev, half, block_size))] * plane,
             [(slot_index, smem)] + [(part, vmem) for part in sources + beside],
             [pltpu.VMEM((len(sources), half, var_dev), f32)],
         )
-        return slots, beside
 
     def deliver(slots):
         routed = list(slots)
@@ -423,7 +419,8 @@
             )
         return routed
 
-    resid_slots, resid_parts = route(resid_near, resid_far, residual)
+    resid_parts = own_rows(residual)
+    resid_slots = gather_slots(exchange(resid_near, 0), exchange(resid_far, 1), resid_parts)
     routed_resid = deliver(resid_slots)
     tiles_hi, tiles_lo = call(
         tile_kernel,
@@ -439,9 +436,9 @@
         estimate=cost(0, 16 * sample_all * var_dev),
     )
 
-    keep, give = call(
+    sides = call(
         functools.partial(product_kernel, x_count),
-        [chip((x_count, sample_dev, var_dev))] * 2,
+        [chip((x_count, half, var_dev))] * 4,
         [
             (row_local, smem),
             (place, smem),
@@ -451,15 +448,21 @@
         + [(part, vmem) for part in routed_resid],
         [pltpu.VMEM((blocks_dev, sample_all, block_size), f32)],
     )
-    got = swap_core(give)
-    arrived = [shift_x(keep[dx] + got[dx], dx) for dx in range(1, x_count)]
-    applied, applied_near, applied_far = call(
-        functools.partial(applied_kernel, len(arrived)),
-        field_outs,
-        [(part, vmem) for part in (keep, got, residual, diagonal, *arrived)],
-    )
-
-    applied_slots, applied_parts = route(applied_near, applied_far, applied)
+    halves, exchanged = [], []
+    for du in range(2):
+        keep, give = sides[2 * du : 2 * du + 2]
+        arrived = []
+        got = swap_core(give)
+        for dx in range(1, x_count):
+            arrived.append(shift_x(keep[dx] + got[dx], dx))
+        halves = call(
+            functools.partial(applied_kernel, du, len(arrived)),
+            [chip((half, var_dev))] + [chip((sample_dev, var_dev))] * du,
+            [(part, vmem) for part in (keep, got, residual, diagonal, *arrived, *halves)],
+        )
+        exchanged.append(exchange(halves[0], du))
+    applied_parts = own_rows(halves[1])
+    applied_slots = gather_slots(*exchanged, applied_parts)
     routed_applied = deliver(applied_slots)
     partial, new_diagonal = call(
         functools.partial(first_kernel, x_count, scale),

time: 121 us -> 119 us (0.983)
  waiting for transfers between devices: 47.1 us -> 39.4 us
  starting transfers between devices: 39.2 us -> 44.7 us
    ppermute x38 -> x40, waiting for transfers between devices: 44.3 us -> 36.7 us  [permute(): lax.ppermute(value, names, [(at, flat(target(*coords_of(at)))) for at in...]
    ppermute x38 -> x40, starting transfers between devices: 31.8 us -> 37.3 us  [permute(): lax.ppermute(value, names, [(at, flat(target(*coords_of(at)))) for at in...]
    pallas_call x11 -> x12, Pallas kernels: 32.5 us -> 32.5 us  [call(): pl.pallas_call(kernel, out_shape=[out for out, _ in outs], in_specs=specs...]
  transfers between devices with their start and end apart: 39 -> 41, of which waited for: 17 -> 17; matrix products, arithmetic and copies ran while one was open for 0% -> 0% of each run, Pallas kernels for 13% -> 13%
where the time goes in v1:
time: 119 us
  starting transfers between devices  44.7 us (38%)
  waiting for transfers between devices  39.4 us (33%)
  Pallas kernels  32.5 us (27%)
  local copies, waits for them, and re-layouts  1.45 us (1%)
    ppermute x40, starting transfers between devices, permute(): lax.ppermute(value, names, [(at, flat(target(*coords_of(at)))) for at in...  37.3 us
    ppermute x40, waiting for transfers between devices, permute(): lax.ppermute(value, names, [(at, flat(target(*coords_of(at)))) for at in...  36.7 us
    pallas_call x12, Pallas kernels, call(): pl.pallas_call(kernel, out_shape=[out for out, _ in outs], in_specs=specs...  32.5 us
    all_to_all x1, starting transfers between devices, per_device(): score_terms = lax.all_to_all(score_copies, ROWS, 0, 0, tiled=True)  7.32 us
    all_to_all x1, waiting for transfers between devices, per_device(): score_terms = lax.all_to_all(score_copies, ROWS, 0, 0, tiled=True)  2.73 us
  transfers between devices with their start and end apart: 41, of which 17 were waited for; matrix products, arithmetic and copies ran while one was open for 0% of the time, Pallas kernels for 13%

profile of v1, /device:TPU:0, one launch (start us, length us, event | category | flops | bytes accessed | tf_op | source)
XLA Modules:
  0.0 118.9 jit_solution(1948531963409788846)
XLA Ops:
  0.6 3.4 %shard_map.77 = (f32[8,16,256]{2,1,0:T(8,128)}, f32[16,4096]{1,0:T(8,128)S(1)}, bf16[256,4096]{1,0:T(8,128)(2,1)S(1)}) custom-call(f32[16,4096]{1,0:T(8,128)} %samples.1, bf16[256,4096]{1,0:T(8,128)(2,1)} %loadings.1), custom_call_target="tpu_custom_call" | custom-call | tf_op jit(solution)/shard_map/pallas_call | solution.py:334
  4.0 7.3 %all-to-all-start = ((f32[8,16,256]{2,1,0:T(8,128)}), f32[8,16,256]{2,1,0:T(8,128)S(1)}, u32[]{:S(2)}, u32[]{:S(2)}) async-start(f32[8,16,256]{2,1,0:T(8,128)} %get-tuple-element.39.after), calls=%async_computation | async-start | bytes 262144 | tf_op jit(solution)/shard_map/all_to_all | solution.py:367
  11.3 0.1 stack.23.place
  11.4 0.7 copy-done.1
  12.1 0.7 copy-done.2
  12.8 3.2 %shard_map.78 = (s32[10]{0:T(128)S(1)}, s32[10]{0:T(128)S(1)}, s32[80]{0:T(128)S(1)}) custom-call(s32[5]{0:T(128)S(1)} %stack.23.place, s32[320]{0:T(512)S(1)} %copy-done.1, s32[320]{0:T(512)S(1)} %copy-done.2, f32[8,16,256]{2,1,0:T(8,128)} %get-tuple-element.39.after), custom_call_target="tpu_custom_call" | custom-call | tf_op jit(solution)/shard_map/pallas_call | solution.py:334
  15.9 2.7 %all-to-all-done.scores = f32[8,16,256]{2,1,0:T(8,128)S(1)} async-done(((f32[8,16,256]{2,1,0:T(8,128)}), f32[8,16,256]{2,1,0:T(8,128)S(1)}, u32[]{:S(2)}, u32[]{:S(2)}) %all-to-all-start) | async-done | bytes 131104 | tf_op jit(solution)/shard_map/all_to_all | solution.py:367
  18.7 1.0 shard_map.79
  19.6 1.6 %collective-permute-start.8 = (f32[16,4096]{1,0:T(8,128)S(1)}, f32[16,4096]{1,0:T(8,128)S(1)}, u32[]{:S(2)}, u32[]{:S(2)}) collective-permute-start(f32[16,4096]{1,0:T(8,128)S(1)} %get-tuple-element.47.refs_8_.refs_0_.refs_2_), channel_id=1, source_target_pairs={{0,2},{2,0},{1,3},{3,1},{4,6},{6,4},{5,7},{7,5},{8,10},{10,8},{9,1... | collective-permute-start | bytes 786440 | tf_op jit(solution)/shard_map/ppermute | solution.py:315
  21.2 0.4 collective-permute-start.4
  21.6 0.7 collective-permute-start
  22.3 1.9 %collective-permute-start.6 = (f32[8,4096]{1,0:T(8,128)S(1)}, f32[8,4096]{1,0:T(8,128)S(1)}, u32[]{:S(2)}, u32[]{:S(2)}) collective-permute-start(f32[8,4096]{1,0:T(8,128)S(1)} %get-tuple-element.46), channel_id=1, source_target_pairs={{0,24},{1,28},{4,25},{5,29},{8,16},{9,20},{12,17},{13,21},{16,8},{... | collective-permute-start | bytes 393224 | tf_op jit(solution)/shard_map/ppermute | solution.py:315
  24.2 1.3 %collective-permute-start.2 = (f32[8,4096]{1,0:T(8,128)S(1)}, f32[8,4096]{1,0:T(8,128)S(1)}, u32[]{:S(2)}, u32[]{:S(2)}) collective-permute-start(f32[8,4096]{1,0:T(8,128)S(1)} %get-tuple-element.46), channel_id=1, source_target_pairs={{0,8},{1,12},{4,9},{5,13},{8,0},{9,4},{12,1},{13,5},{16,24},{17,28... | collective-permute-start | bytes 393224 | tf_op jit(solution)/shard_map/ppermute | solution.py:315
  25.4 8.1 %collective-permute-done.4.refs_4_ = f32[8,4096]{1,0:T(8,128)S(1)} collective-permute-done((f32[8,4096]{1,0:T(8,128)S(1)}, f32[8,4096]{1,0:T(8,128)S(1)}, u32[]{:S(2)}, u32[]{:S(2)}) %collective-permute-start.4) | collective-permute-done | bytes 131104 | tf_op jit(solution)/shard_map/ppermute | solution.py:315
  33.5 0.5 collective-permute-start.9
  34.1 0.4 collective-permute-start.1
  34.6 1.0 collective-permute-done.2.refs_2_
  35.6 0.5 collective-permute-start.3
  36.1 0.8 collective-permute-done.7.refs_7_
  36.9 0.2 collective-permute-done.3.refs_3_
  37.1 1.1 shard_map.80
  38.2 0.6 collective-permute-start.11
  38.8 1.7 %collective-permute-start.12 = (f32[10,8,512]{2,1,0:T(8,128)S(1)}, f32[10,8,512]{2,1,0:T(8,128)S(1)}, u32[]{:S(2)}, u32[]{:S(2)}) collective-permute-start(f32[10,8,512]{2,1,0:T(8,128)S(1)} %get-tuple-element.54), channel_id=1, source_target_pairs={{0,4},{2,6},{4,0},{6,2},{8,12},{10,14},{12,8},{14,10},{1,5},{3,7},... | collective-permute-start | bytes 491528 | tf_op jit(solution)/shard_map/ppermute | solution.py:315
  40.6 1.2 %collective-permute-start.13 = (f32[10,8,512]{2,1,0:T(8,128)S(1)}, f32[10,8,512]{2,1,0:T(8,128)S(1)}, u32[]{:S(2)}, u32[]{:S(2)}) collective-permute-start(f32[10,8,512]{2,1,0:T(8,128)S(1)} %get-tuple-element.55), channel_id=1, source_target_pairs={{0,6},{2,4},{4,2},{6,0},{8,14},{10,12},{12,10},{14,8},{1,7},{3,5},... | collective-permute-start | bytes 491528 | tf_op jit(solution)/shard_map/ppermute | solution.py:315
  41.8 1.3 %collective-permute-start.14 = (f32[10,8,512]{2,1,0:T(8,128)S(1)}, f32[10,8,512]{2,1,0:T(8,128)S(1)}, u32[]{:S(2)}, u32[]{:S(2)}) collective-permute-start(f32[10,8,512]{2,1,0:T(8,128)S(1)} %get-tuple-element.56), channel_id=1, source_target_pairs={{0,8},{2,10},{4,12},{6,14},{8,0},{10,2},{12,4},{14,6},{1,9},{3,11}... | collective-permute-start | bytes 491528 | tf_op jit(solution)/shard_map/ppermute | solution.py:315
  43.1 0.6 collective-permute-start.15
  43.8 1.6 %collective-permute-done.11.refs_1_.refs_5_ = f32[10,8,512]{2,1,0:T(8,128)S(1)} collective-permute-done((f32[10,8,512]{2,1,0:T(8,128)S(1)}, f32[10,8,512]{2,1,0:T(8,128)S(1)}, u32[]{:S(2)}, u32[]{:S(2)}) %collective-permute-start.11) | collective-permute-done | bytes 163872 | tf_op jit(solution)/shard_map/ppermute | solution.py:315
  45.4 1.9 %collective-permute-start.16 = (f32[10,8,512]{2,1,0:T(8,128)S(1)}, f32[10,8,512]{2,1,0:T(8,128)S(1)}, u32[]{:S(2)}, u32[]{:S(2)}) collective-permute-start(f32[10,8,512]{2,1,0:T(8,128)S(1)} %get-tuple-element.58), channel_id=1, source_target_pairs={{0,12},{2,14},{4,8},{6,10},{8,4},{10,6},{12,0},{14,2},{1,13},{3,15... | collective-permute-start | bytes 491528 | tf_op jit(solution)/shard_map/ppermute | solution.py:315
  47.3 3.1 %collective-permute-start.17 = (f32[10,8,512]{2,1,0:T(8,128)S(1)}, f32[10,8,512]{2,1,0:T(8,128)S(1)}, u32[]{:S(2)}, u32[]{:S(2)}) collective-permute-start(f32[10,8,512]{2,1,0:T(8,128)S(1)} %get-tuple-element.59), channel_id=1, source_target_pairs={{0,14},{2,12},{4,10},{6,8},{8,6},{10,4},{12,2},{14,0},{1,15},{3,13... | collective-permute-start | bytes 491528 | tf_op jit(solution)/shard_map/ppermute | solution.py:315
  50.4 4.8 %shard_map.82 = (bf16[10,512,512]{2,1,0:T(8,128)(2,1)S(1)}, bf16[10,512,512]{2,1,0:T(8,128)(2,1)S(1)}) custom-call(s32[10]{0:T(128)S(1)} %get-tuple-element.41.is_diag, f32[10,512,512]{2,1,0:T(8,128)} %tiles.3, f32[10,8,512]{2,1,0:T(8,128)S(1)} %get-tuple-element.48.after.refs_0_.refs_4_), custom_call_target="tpu_custom_call" | custom-call | bytes 20971520 | tf_op jit(solution)/shard_map/pallas_call | solution.py:334
  55.3 1.8 %collective-permute-done.16.refs_6_.refs_10_ = f32[10,8,512]{2,1,0:T(8,128)S(1)} collective-permute-done((f32[10,8,512]{2,1,0:T(8,128)S(1)}, f32[10,8,512]{2,1,0:T(8,128)S(1)}, u32[]{:S(2)}, u32[]{:S(2)}) %collective-permute-start.16) | collective-permute-done | bytes 163872 | tf_op jit(solution)/shard_map/ppermute | solution.py:315
  57.1 2.0 %collective-permute-done.17.refs_7_.refs_11_ = f32[10,8,512]{2,1,0:T(8,128)S(1)} collective-permute-done((f32[10,8,512]{2,1,0:T(8,128)S(1)}, f32[10,8,512]{2,1,0:T(8,128)S(1)}, u32[]{:S(2)}, u32[]{:S(2)}) %collective-permute-start.17) | collective-permute-done | bytes 163872 | tf_op jit(solution)/shard_map/ppermute | solution.py:315
  59.1 5.2 %shard_map.83 = (f32[2,8,4096]{2,1,0:T(8,128)S(1)}, f32[2,8,4096]{2,1,0:T(8,128)S(1)}, f32[2,8,4096]{2,1,0:T(8,128)S(1)}, f32[2,8,4096]{2,1,0:T(8,128)S(1)}) custom-call(s32[10]{0:T(128)S(1)} %get-tuple-element.40.row_local, s32[5]{0:T(128)S(1)} %stack.23.place, bf16[10,512,512]{2,1,0:T(8,128)(2,1)S(1)} %get-tuple-element.51.tile_hi, ...), custom_call_target="tpu_custom_call" | custom-call | tf_op jit(solution)/shard_map/pallas_call | solution.py:334
  64.4 0.5 collective-permute-start.22
  64.9 1.0 collective-permute-done.18.refs_1_
  65.9 1.5 %collective-permute-start.19 = (f32[8,4096]{1,0:T(8,128)S(1)}, f32[8,4096]{1,0:T(8,128)S(1)}, u32[]{:S(2)}, u32[]{:S(2)}) collective-permute-start(f32[8,4096]{1,0:T(8,128)S(1)} %fusion.1), channel_id=1, source_target_pairs={{0,2},{2,0},{1,3},{3,1},{4,6},{6,4},{5,7},{7,5},{8,10},{10,8},{9,1... | collective-permute-start | bytes 393224 | tf_op jit(solution)/shard_map/ppermute | solution.py:315
  67.5 0.6 collective-permute-start.23
  68.1 4.3 %collective-permute-done.19.refs_4_ = f32[8,4096]{1,0:T(8,128)S(1)} collective-permute-done((f32[8,4096]{1,0:T(8,128)S(1)}, f32[8,4096]{1,0:T(8,128)S(1)}, u32[]{:S(2)}, u32[]{:S(2)}) %collective-permute-start.19) | collective-permute-done | bytes 131104 | tf_op jit(solution)/shard_map/ppermute | solution.py:315
  72.4 1.9 %collective-permute-done.23.refs_4_ = f32[8,4096]{1,0:T(8,128)S(1)} collective-permute-done((f32[8,4096]{1,0:T(8,128)S(1)}, f32[8,4096]{1,0:T(8,128)S(1)}, u32[]{:S(2)}, u32[]{:S(2)}) %collective-permute-start.23) | collective-permute-done | bytes 131104 | tf_op jit(solution)/shard_map/ppermute | solution.py:315
  74.4 1.5 %collective-permute-start.30 = (f32[16,4096]{1,0:T(8,128)S(1)}, f32[16,4096]{1,0:T(8,128)S(1)}, u32[]{:S(2)}, u32[]{:S(2)}) collective-permute-start(f32[16,4096]{1,0:T(8,128)S(1)} %get-tuple-element.65.refs_8_.refs_0_), channel_id=1, source_target_pairs={{0,2},{2,0},{1,3},{3,1},{4,6},{6,4},{5,7},{7,5},{8,10},{10,8},{9,1... | collective-permute-start | bytes 786440 | tf_op jit(solution)/shard_map/ppermute | solution.py:315
  75.9 1.5 %collective-permute-start.26 = (f32[8,4096]{1,0:T(8,128)S(1)}, f32[8,4096]{1,0:T(8,128)S(1)}, u32[]{:S(2)}, u32[]{:S(2)}) collective-permute-start(f32[8,4096]{1,0:T(8,128)S(1)} %shard_map.84.refs_5_), channel_id=1, source_target_pairs={{0,16},{1,20},{4,17},{5,21},{8,24},{9,28},{12,25},{13,29},{16,0},{... | collective-permute-start | bytes 393224 | tf_op jit(solution)/shard_map/ppermute | solution.py:315
  77.4 0.7 collective-permute-start.20
  78.1 1.5 %collective-permute-start.28 = (f32[8,4096]{1,0:T(8,128)S(1)}, f32[8,4096]{1,0:T(8,128)S(1)}, u32[]{:S(2)}, u32[]{:S(2)}) collective-permute-start(f32[8,4096]{1,0:T(8,128)S(1)} %get-tuple-element.64), channel_id=1, source_target_pairs={{0,24},{1,28},{4,25},{5,29},{8,16},{9,20},{12,17},{13,21},{16,8},{... | collective-permute-start | bytes 393224 | tf_op jit(solution)/shard_map/ppermute | solution.py:315
  79.6 0.5 collective-permute-start.24
  80.1 8.6 %collective-permute-done.26.refs_4_ = f32[8,4096]{1,0:T(8,128)S(1)} collective-permute-done((f32[8,4096]{1,0:T(8,128)S(1)}, f32[8,4096]{1,0:T(8,128)S(1)}, u32[]{:S(2)}, u32[]{:S(2)}) %collective-permute-start.26) | collective-permute-done | bytes 131104 | tf_op jit(solution)/shard_map/ppermute | solution.py:315
  88.8 0.5 collective-permute-start.31
  89.4 0.4 collective-permute-start.21
  89.8 0.9 collective-permute-done.24.refs_2_
  90.7 0.5 collective-permute-start.25
  91.2 0.8 collective-permute-done.29.refs_7_
  92.0 0.2 collective-permute-done.25.refs_3_
  92.2 1.1 shard_map.86
  93.4 0.6 collective-permute-start.33
  94.0 1.6 %collective-permute-start.34 = (f32[10,8,512]{2,1,0:T(8,128)S(1)}, f32[10,8,512]{2,1,0:T(8,128)S(1)}, u32[]{:S(2)}, u32[]{:S(2)}) collective-permute-start(f32[10,8,512]{2,1,0:T(8,128)S(1)} %get-tuple-element.69), channel_id=1, source_target_pairs={{0,4},{2,6},{4,0},{6,2},{8,12},{10,14},{12,8},{14,10},{1,5},{3,7},... | collective-permute-start | bytes 491528 | tf_op jit(solution)/shard_map/ppermute | solution.py:315
  95.6 1.4 %collective-permute-start.35 = (f32[10,8,512]{2,1,0:T(8,128)S(1)}, f32[10,8,512]{2,1,0:T(8,128)S(1)}, u32[]{:S(2)}, u32[]{:S(2)}) collective-permute-start(f32[10,8,512]{2,1,0:T(8,128)S(1)} %get-tuple-element.70), channel_id=1, source_target_pairs={{0,6},{2,4},{4,2},{6,0},{8,14},{10,12},{12,10},{14,8},{1,7},{3,5},... | collective-permute-start | bytes 491528 | tf_op jit(solution)/shard_map/ppermute | solution.py:315
  96.9 1.0 collective-permute-start.36
  98.0 1.0 collective-permute-start.37
  99.0 1.6 %collective-permute-done.33.refs_1_ = f32[10,8,512]{2,1,0:T(8,128)S(1)} collective-permute-done((f32[10,8,512]{2,1,0:T(8,128)S(1)}, f32[10,8,512]{2,1,0:T(8,128)S(1)}, u32[]{:S(2)}, u32[]{:S(2)}) %collective-permute-start.33) | collective-permute-done | bytes 163872 | tf_op jit(solution)/shard_map/ppermute | solution.py:315
  100.5 1.2 %collective-permute-start.38 = (f32[10,8,512]{2,1,0:T(8,128)S(1)}, f32[10,8,512]{2,1,0:T(8,128)S(1)}, u32[]{:S(2)}, u32[]{:S(2)}) collective-permute-start(f32[10,8,512]{2,1,0:T(8,128)S(1)} %get-tuple-element.73), channel_id=1, source_target_pairs={{0,12},{2,14},{4,8},{6,10},{8,4},{10,6},{12,0},{14,2},{1,13},{3,15... | collective-permute-start | bytes 491528 | tf_op jit(solution)/shard_map/ppermute | solution.py:315
  101.7 2.7 %collective-permute-start.39 = (f32[10,8,512]{2,1,0:T(8,128)S(1)}, f32[10,8,512]{2,1,0:T(8,128)S(1)}, u32[]{:S(2)}, u32[]{:S(2)}) collective-permute-start(f32[10,8,512]{2,1,0:T(8,128)S(1)} %get-tuple-element.74), channel_id=1, source_target_pairs={{0,14},{2,12},{4,10},{6,8},{8,6},{10,4},{12,2},{14,0},{1,15},{3,13... | collective-permute-start | bytes 491528 | tf_op jit(solution)/shard_map/ppermute | solution.py:315
  104.4 1.5 %shard_map.81 = (f32[64,4096]{1,0:T(8,128)S(1)}, bf16[8,512,192]{2,1,0:T(8,128)(2,1)S(1)}) custom-call(s32[5]{0:T(128)S(1)} %stack.23.place, f32[10,8,512]{2,1,0:T(8,128)S(1)} %get-tuple-element.48.after.refs_0_.refs_4_, f32[16,4096]{1,0:T(8,128)S(1)} %get-tuple-element.47.refs_8_.refs_0_.refs_2_, f32[16,4096]{1,0:T(8,128)S(1)} %collective-permute-done.8.refs_9_.refs_1_, ...), custom_call_target="tpu_custom_call" | custom-call | bytes 4194304 | tf_op jit(solution)/shard_map/pallas_call | solution.py:334
  105.9 6.3 %shard_map.87 = (f32[10,512,512]{2,1,0:T(8,128)S(1)}, f32[1,4096]{1,0:T(1,128)}) custom-call(s32[10]{0:T(128)S(1)} %get-tuple-element.40.row_local, s32[5]{0:T(128)S(1)} %stack.23.place, f32[10,512,512]{2,1,0:T(8,128)} %tiles.3, f32[1,4096]{1,0:T(1,128)S(1)} %bitcast.13, f32[64,4096]{1,0:T(8,128)S(1)} %get-tuple-element.50.resid_rows, ...), custom_call_target="tpu_custom_call" | custom-call | flops 1006632960 | bytes 41943040 | tf_op jit(solution)/shard_map/pallas_call | solution.py:334
  112.2 1.8 %collective-permute-done.39.refs_7_ = f32[10,8,512]{2,1,0:T(8,128)S(1)} collective-permute-done((f32[10,8,512]{2,1,0:T(8,128)S(1)}, f32[10,8,512]{2,1,0:T(8,128)S(1)}, u32[]{:S(2)}, u32[]{:S(2)}) %collective-permute-start.39) | collective-permute-done | bytes 163872 | tf_op jit(solution)/shard_map/ppermute | solution.py:315
  114.0 4.8 %shard_map.88 = f32[10,512,512]{2,1,0:T(8,128)} custom-call(s32[10]{0:T(128)S(1)} %get-tuple-element.40.row_local, s32[10]{0:T(128)S(1)} %get-tuple-element.41.is_diag, bf16[8,512,192]{2,1,0:T(8,128)(2,1)S(1)} %get-tuple-element.49.left, f32[10,512,512]{2,1,0:T(8,128)S(1)} %get-tuple-element.67.partial, f32[10,8,512]{2,1,0:T(8,128)S(1)} %get-tuple-element.66.after.refs_0_, ...), custom_call_target="tpu_custom_call" | custom-call | tf_op jit(solution)/shard_map/pallas_call | solution.py:334
  (39 shorter events, 0.4 us)
Async XLA Ops:
  4.0 14.7 %all-to-all-start = ((f32[8,16,256]{2,1,0:T(8,128)}), f32[8,16,256]{2,1,0:T(8,128)S(1)}, u32[]{:S(2)}, u32[]{:S(2)}) async-start(f32[8,16,256]{2,1,0:T(8,128)} %get-tuple-element.39.after), calls=%async_computation | async-start | bytes 262144 | tf_op jit(solution)/shard_map/all_to_all | solution.py:367
  11.4 0.7 copy-start.1
  12.1 0.7 copy-start.2
  19.6 14.4 %collective-permute-start.8 = (f32[16,4096]{1,0:T(8,128)S(1)}, f32[16,4096]{1,0:T(8,128)S(1)}, u32[]{:S(2)}, u32[]{:S(2)}) collective-permute-start(f32[16,4096]{1,0:T(8,128)S(1)} %get-tuple-element.47.refs_8_.refs_0_.refs_2_), channel_id=1, source_target_pairs={{0,2},{2,0},{1,3},{3,1},{4,6},{6,4},{5,7},{7,5},{8,10},{10,8},{9,1... | collective-permute-start | bytes 786440 | tf_op jit(solution)/shard_map/ppermute | solution.py:315
  21.2 12.3 %collective-permute-start.4 = (f32[8,4096]{1,0:T(8,128)S(1)}, f32[8,4096]{1,0:T(8,128)S(1)}, u32[]{:S(2)}, u32[]{:S(2)}) collective-permute-start(f32[8,4096]{1,0:T(8,128)S(1)} %get-tuple-element.45), channel_id=1, source_target_pairs={{0,16},{1,20},{4,17},{5,21},{8,24},{9,28},{12,25},{13,29},{16,0},{... | collective-permute-start | bytes 393224 | tf_op jit(solution)/shard_map/ppermute | solution.py:315
  21.6 11.9 %collective-permute-start = (f32[8,4096]{1,0:T(8,128)S(1)}, f32[8,4096]{1,0:T(8,128)S(1)}, u32[]{:S(2)}, u32[]{:S(2)}) collective-permute-start(f32[8,4096]{1,0:T(8,128)S(1)} %get-tuple-element.45), channel_id=1, source_target_pairs={{0,0},{1,4},{4,1},{5,5},{8,8},{9,12},{12,9},{13,13},{16,16},{17,20... | collective-permute-start | bytes 393224 | tf_op jit(solution)/shard_map/ppermute | solution.py:315
  22.3 11.9 %collective-permute-start.6 = (f32[8,4096]{1,0:T(8,128)S(1)}, f32[8,4096]{1,0:T(8,128)S(1)}, u32[]{:S(2)}, u32[]{:S(2)}) collective-permute-start(f32[8,4096]{1,0:T(8,128)S(1)} %get-tuple-element.46), channel_id=1, source_target_pairs={{0,24},{1,28},{4,25},{5,29},{8,16},{9,20},{12,17},{13,21},{16,8},{... | collective-permute-start | bytes 393224 | tf_op jit(solution)/shard_map/ppermute | solution.py:315
  24.2 11.4 %collective-permute-start.2 = (f32[8,4096]{1,0:T(8,128)S(1)}, f32[8,4096]{1,0:T(8,128)S(1)}, u32[]{:S(2)}, u32[]{:S(2)}) collective-permute-start(f32[8,4096]{1,0:T(8,128)S(1)} %get-tuple-element.46), channel_id=1, source_target_pairs={{0,8},{1,12},{4,9},{5,13},{8,0},{9,4},{12,1},{13,5},{16,24},{17,28... | collective-permute-start | bytes 393224 | tf_op jit(solution)/shard_map/ppermute | solution.py:315
  33.5 2.0 %collective-permute-start.5 = (f32[8,4096]{1,0:T(8,128)S(1)}, f32[8,4096]{1,0:T(8,128)S(1)}, u32[]{:S(2)}, u32[]{:S(2)}) collective-permute-start(f32[8,4096]{1,0:T(8,128)S(1)} %collective-permute-done.4.refs_4_), channel_id=1, source_target_pairs={{0,1},{1,0},{2,3},{3,2},{4,5},{5,4},{6,7},{7,6},{8,9},{9,8},{10,11... | collective-permute-start | bytes 393224 | tf_op jit(solution)/shard_map/ppermute | solution.py:315
  33.5 3.6 %collective-permute-start.9 = (f32[16,4096]{1,0:T(8,128)S(1)}, f32[16,4096]{1,0:T(8,128)S(1)}, u32[]{:S(2)}, u32[]{:S(2)}) collective-permute-start(f32[16,4096]{1,0:T(8,128)S(1)} %get-tuple-element.47.refs_8_.refs_0_.refs_2_), channel_id=1, source_target_pairs={{0,1},{1,0},{2,3},{3,2},{4,5},{5,4},{6,7},{7,6},{8,9},{9,8},{10,11... | collective-permute-start | bytes 786440 | tf_op jit(solution)/shard_map/ppermute | solution.py:315
  34.1 3.1 %collective-permute-start.10 = (f32[16,4096]{1,0:T(8,128)S(1)}, f32[16,4096]{1,0:T(8,128)S(1)}, u32[]{:S(2)}, u32[]{:S(2)}) collective-permute-start(f32[16,4096]{1,0:T(8,128)S(1)} %collective-permute-done.8.refs_9_.refs_1_), channel_id=1, source_target_pairs={{0,1},{1,0},{2,3},{3,2},{4,5},{5,4},{6,7},{7,6},{8,9},{9,8},{10,11... | collective-permute-start | bytes 786440 | tf_op jit(solution)/shard_map/ppermute | solution.py:315
  34.1 2.0 %collective-permute-start.1 = (f32[8,4096]{1,0:T(8,128)S(1)}, f32[8,4096]{1,0:T(8,128)S(1)}, u32[]{:S(2)}, u32[]{:S(2)}) collective-permute-start(f32[8,4096]{1,0:T(8,128)S(1)} %collective-permute-done.refs_0_), channel_id=1, source_target_pairs={{0,1},{1,0},{2,3},{3,2},{4,5},{5,4},{6,7},{7,6},{8,9},{9,8},{10,11... | collective-permute-start | bytes 393224 | tf_op jit(solution)/shard_map/ppermute | solution.py:315
  35.6 1.3 %collective-permute-start.7 = (f32[8,4096]{1,0:T(8,128)S(1)}, f32[8,4096]{1,0:T(8,128)S(1)}, u32[]{:S(2)}, u32[]{:S(2)}) collective-permute-start(f32[8,4096]{1,0:T(8,128)S(1)} %collective-permute-done.6.refs_6_), channel_id=1, source_target_pairs={{0,1},{1,0},{2,3},{3,2},{4,5},{5,4},{6,7},{7,6},{8,9},{9,8},{10,11... | collective-permute-start | bytes 393224 | tf_op jit(solution)/shard_map/ppermute | solution.py:315
  35.6 1.5 %collective-permute-start.3 = (f32[8,4096]{1,0:T(8,128)S(1)}, f32[8,4096]{1,0:T(8,128)S(1)}, u32[]{:S(2)}, u32[]{:S(2)}) collective-permute-start(f32[8,4096]{1,0:T(8,128)S(1)} %collective-permute-done.2.refs_2_), channel_id=1, source_target_pairs={{0,1},{1,0},{2,3},{3,2},{4,5},{5,4},{6,7},{7,6},{8,9},{9,8},{10,11... | collective-permute-start | bytes 393224 | tf_op jit(solution)/shard_map/ppermute | solution.py:315
  38.2 7.1 %collective-permute-start.11 = (f32[10,8,512]{2,1,0:T(8,128)S(1)}, f32[10,8,512]{2,1,0:T(8,128)S(1)}, u32[]{:S(2)}, u32[]{:S(2)}) collective-permute-start(f32[10,8,512]{2,1,0:T(8,128)S(1)} %get-tuple-element.53), channel_id=1, source_target_pairs={{0,2},{2,0},{4,6},{6,4},{8,10},{10,8},{12,14},{14,12},{1,3},{3,1},... | collective-permute-start | bytes 491528 | tf_op jit(solution)/shard_map/ppermute | solution.py:315
  38.8 8.5 %collective-permute-start.12 = (f32[10,8,512]{2,1,0:T(8,128)S(1)}, f32[10,8,512]{2,1,0:T(8,128)S(1)}, u32[]{:S(2)}, u32[]{:S(2)}) collective-permute-start(f32[10,8,512]{2,1,0:T(8,128)S(1)} %get-tuple-element.54), channel_id=1, source_target_pairs={{0,4},{2,6},{4,0},{6,2},{8,12},{10,14},{12,8},{14,10},{1,5},{3,7},... | collective-permute-start | bytes 491528 | tf_op jit(solution)/shard_map/ppermute | solution.py:315
  40.6 14.7 %collective-permute-start.13 = (f32[10,8,512]{2,1,0:T(8,128)S(1)}, f32[10,8,512]{2,1,0:T(8,128)S(1)}, u32[]{:S(2)}, u32[]{:S(2)}) collective-permute-start(f32[10,8,512]{2,1,0:T(8,128)S(1)} %get-tuple-element.55), channel_id=1, source_target_pairs={{0,6},{2,4},{4,2},{6,0},{8,14},{10,12},{12,10},{14,8},{1,7},{3,5},... | collective-permute-start | bytes 491528 | tf_op jit(solution)/shard_map/ppermute | solution.py:315
  41.8 13.5 %collective-permute-start.14 = (f32[10,8,512]{2,1,0:T(8,128)S(1)}, f32[10,8,512]{2,1,0:T(8,128)S(1)}, u32[]{:S(2)}, u32[]{:S(2)}) collective-permute-start(f32[10,8,512]{2,1,0:T(8,128)S(1)} %get-tuple-element.56), channel_id=1, source_target_pairs={{0,8},{2,10},{4,12},{6,14},{8,0},{10,2},{12,4},{14,6},{1,9},{3,11}... | collective-permute-start | bytes 491528 | tf_op jit(solution)/shard_map/ppermute | solution.py:315
  43.1 12.1 %collective-permute-start.15 = (f32[10,8,512]{2,1,0:T(8,128)S(1)}, f32[10,8,512]{2,1,0:T(8,128)S(1)}, u32[]{:S(2)}, u32[]{:S(2)}) collective-permute-start(f32[10,8,512]{2,1,0:T(8,128)S(1)} %get-tuple-element.57), channel_id=1, source_target_pairs={{0,10},{2,8},{4,14},{6,12},{8,2},{10,0},{12,6},{14,4},{1,11},{3,9}... | collective-permute-start | bytes 491528 | tf_op jit(solution)/shard_map/ppermute | solution.py:315
  45.4 11.7 %collective-permute-start.16 = (f32[10,8,512]{2,1,0:T(8,128)S(1)}, f32[10,8,512]{2,1,0:T(8,128)S(1)}, u32[]{:S(2)}, u32[]{:S(2)}) collective-permute-start(f32[10,8,512]{2,1,0:T(8,128)S(1)} %get-tuple-element.58), channel_id=1, source_target_pairs={{0,12},{2,14},{4,8},{6,10},{8,4},{10,6},{12,0},{14,2},{1,13},{3,15... | collective-permute-start | bytes 491528 | tf_op jit(solution)/shard_map/ppermute | solution.py:315
  47.3 11.8 %collective-permute-start.17 = (f32[10,8,512]{2,1,0:T(8,128)S(1)}, f32[10,8,512]{2,1,0:T(8,128)S(1)}, u32[]{:S(2)}, u32[]{:S(2)}) collective-permute-start(f32[10,8,512]{2,1,0:T(8,128)S(1)} %get-tuple-element.59), channel_id=1, source_target_pairs={{0,14},{2,12},{4,10},{6,8},{8,6},{10,4},{12,2},{14,0},{1,15},{3,13... | collective-permute-start | bytes 491528 | tf_op jit(solution)/shard_map/ppermute | solution.py:315
  59.1 13.3 %copy-start = (f32[4096]{0:T(1024)S(1)}, f32[4096]{0:T(1024)}, u32[]{:S(2)}) copy-start(f32[4096]{0:T(1024)} %param.9) | copy-start | bytes 49156
  64.3 1.6 %collective-permute-start.18 = (f32[2,8,4096]{2,1,0:T(8,128)S(1)}, f32[2,8,4096]{2,1,0:T(8,128)S(1)}, u32[]{:S(2)}, u32[]{:S(2)}) collective-permute-start(f32[2,8,4096]{2,1,0:T(8,128)S(1)} %get-tuple-element.61), channel_id=1, source_target_pairs={{0,1},{1,0},{2,3},{3,2},{4,5},{5,4},{6,7},{7,6},{8,9},{9,8},{10,11... | collective-permute-start | bytes 786440 | tf_op jit(solution)/shard_map/ppermute | solution.py:315
  64.4 3.1 %collective-permute-start.22 = (f32[2,8,4096]{2,1,0:T(8,128)S(1)}, f32[2,8,4096]{2,1,0:T(8,128)S(1)}, u32[]{:S(2)}, u32[]{:S(2)}) collective-permute-start(f32[2,8,4096]{2,1,0:T(8,128)S(1)} %get-tuple-element.63), channel_id=1, source_target_pairs={{0,1},{1,0},{2,3},{3,2},{4,5},{5,4},{6,7},{7,6},{8,9},{9,8},{10,11... | collective-permute-start | bytes 786440 | tf_op jit(solution)/shard_map/ppermute | solution.py:315
  65.9 6.4 %collective-permute-start.19 = (f32[8,4096]{1,0:T(8,128)S(1)}, f32[8,4096]{1,0:T(8,128)S(1)}, u32[]{:S(2)}, u32[]{:S(2)}) collective-permute-start(f32[8,4096]{1,0:T(8,128)S(1)} %fusion.1), channel_id=1, source_target_pairs={{0,2},{2,0},{1,3},{3,1},{4,6},{6,4},{5,7},{7,5},{8,10},{10,8},{9,1... | collective-permute-start | bytes 393224 | tf_op jit(solution)/shard_map/ppermute | solution.py:315
  67.5 6.9 %collective-permute-start.23 = (f32[8,4096]{1,0:T(8,128)S(1)}, f32[8,4096]{1,0:T(8,128)S(1)}, u32[]{:S(2)}, u32[]{:S(2)}) collective-permute-start(f32[8,4096]{1,0:T(8,128)S(1)} %fusion), channel_id=1, source_target_pairs={{0,2},{2,0},{1,3},{3,1},{4,6},{6,4},{5,7},{7,5},{8,10},{10,8},{9,1... | collective-permute-start | bytes 393224 | tf_op jit(solution)/shard_map/ppermute | solution.py:315
  74.4 14.9 %collective-permute-start.30 = (f32[16,4096]{1,0:T(8,128)S(1)}, f32[16,4096]{1,0:T(8,128)S(1)}, u32[]{:S(2)}, u32[]{:S(2)}) collective-permute-start(f32[16,4096]{1,0:T(8,128)S(1)} %get-tuple-element.65.refs_8_.refs_0_), channel_id=1, source_target_pairs={{0,2},{2,0},{1,3},{3,1},{4,6},{6,4},{5,7},{7,5},{8,10},{10,8},{9,1... | collective-permute-start | bytes 786440 | tf_op jit(solution)/shard_map/ppermute | solution.py:315
  75.9 12.8 %collective-permute-start.26 = (f32[8,4096]{1,0:T(8,128)S(1)}, f32[8,4096]{1,0:T(8,128)S(1)}, u32[]{:S(2)}, u32[]{:S(2)}) collective-permute-start(f32[8,4096]{1,0:T(8,128)S(1)} %shard_map.84.refs_5_), channel_id=1, source_target_pairs={{0,16},{1,20},{4,17},{5,21},{8,24},{9,28},{12,25},{13,29},{16,0},{... | collective-permute-start | bytes 393224 | tf_op jit(solution)/shard_map/ppermute | solution.py:315
  77.4 11.3 %collective-permute-start.20 = (f32[8,4096]{1,0:T(8,128)S(1)}, f32[8,4096]{1,0:T(8,128)S(1)}, u32[]{:S(2)}, u32[]{:S(2)}) collective-permute-start(f32[8,4096]{1,0:T(8,128)S(1)} %shard_map.84.refs_5_), channel_id=1, source_target_pairs={{0,0},{1,4},{4,1},{5,5},{8,8},{9,12},{12,9},{13,13},{16,16},{17,20... | collective-permute-start | bytes 393224 | tf_op jit(solution)/shard_map/ppermute | solution.py:315
  78.1 11.2 %collective-permute-start.28 = (f32[8,4096]{1,0:T(8,128)S(1)}, f32[8,4096]{1,0:T(8,128)S(1)}, u32[]{:S(2)}, u32[]{:S(2)}) collective-permute-start(f32[8,4096]{1,0:T(8,128)S(1)} %get-tuple-element.64), channel_id=1, source_target_pairs={{0,24},{1,28},{4,25},{5,29},{8,16},{9,20},{12,17},{13,21},{16,8},{... | collective-permute-start | bytes 393224 | tf_op jit(solution)/shard_map/ppermute | solution.py:315
  79.6 11.1 %collective-permute-start.24 = (f32[8,4096]{1,0:T(8,128)S(1)}, f32[8,4096]{1,0:T(8,128)S(1)}, u32[]{:S(2)}, u32[]{:S(2)}) collective-permute-start(f32[8,4096]{1,0:T(8,128)S(1)} %get-tuple-element.64), channel_id=1, source_target_pairs={{0,8},{1,12},{4,9},{5,13},{8,0},{9,4},{12,1},{13,5},{16,24},{17,28... | collective-permute-start | bytes 393224 | tf_op jit(solution)/shard_map/ppermute | solution.py:315
  88.8 1.9 %collective-permute-start.27 = (f32[8,4096]{1,0:T(8,128)S(1)}, f32[8,4096]{1,0:T(8,128)S(1)}, u32[]{:S(2)}, u32[]{:S(2)}) collective-permute-start(f32[8,4096]{1,0:T(8,128)S(1)} %collective-permute-done.26.refs_4_), channel_id=1, source_target_pairs={{0,1},{1,0},{2,3},{3,2},{4,5},{5,4},{6,7},{7,6},{8,9},{9,8},{10,11... | collective-permute-start | bytes 393224 | tf_op jit(solution)/shard_map/ppermute | solution.py:315
  88.8 3.5 %collective-permute-start.31 = (f32[16,4096]{1,0:T(8,128)S(1)}, f32[16,4096]{1,0:T(8,128)S(1)}, u32[]{:S(2)}, u32[]{:S(2)}) collective-permute-start(f32[16,4096]{1,0:T(8,128)S(1)} %get-tuple-element.65.refs_8_.refs_0_), channel_id=1, source_target_pairs={{0,1},{1,0},{2,3},{3,2},{4,5},{5,4},{6,7},{7,6},{8,9},{9,8},{10,11... | collective-permute-start | bytes 786440 | tf_op jit(solution)/shard_map/ppermute | solution.py:315
  89.3 3.0 %collective-permute-start.32 = (f32[16,4096]{1,0:T(8,128)S(1)}, f32[16,4096]{1,0:T(8,128)S(1)}, u32[]{:S(2)}, u32[]{:S(2)}) collective-permute-start(f32[16,4096]{1,0:T(8,128)S(1)} %collective-permute-done.30.refs_9_.refs_1_), channel_id=1, source_target_pairs={{0,1},{1,0},{2,3},{3,2},{4,5},{5,4},{6,7},{7,6},{8,9},{9,8},{10,11... | collective-permute-start | bytes 786440 | tf_op jit(solution)/shard_map/ppermute | solution.py:315
  89.4 1.9 %collective-permute-start.21 = (f32[8,4096]{1,0:T(8,128)S(1)}, f32[8,4096]{1,0:T(8,128)S(1)}, u32[]{:S(2)}, u32[]{:S(2)}) collective-permute-start(f32[8,4096]{1,0:T(8,128)S(1)} %collective-permute-done.20.refs_0_), channel_id=1, source_target_pairs={{0,1},{1,0},{2,3},{3,2},{4,5},{5,4},{6,7},{7,6},{8,9},{9,8},{10,11... | collective-permute-start | bytes 393224 | tf_op jit(solution)/shard_map/ppermute | solution.py:315
  90.7 1.3 %collective-permute-start.29 = (f32[8,4096]{1,0:T(8,128)S(1)}, f32[8,4096]{1,0:T(8,128)S(1)}, u32[]{:S(2)}, u32[]{:S(2)}) collective-permute-start(f32[8,4096]{1,0:T(8,128)S(1)} %collective-permute-done.28.refs_6_), channel_id=1, source_target_pairs={{0,1},{1,0},{2,3},{3,2},{4,5},{5,4},{6,7},{7,6},{8,9},{9,8},{10,11... | collective-permute-start | bytes 393224 | tf_op jit(solution)/shard_map/ppermute | solution.py:315
  90.7 1.5 %collective-permute-start.25 = (f32[8,4096]{1,0:T(8,128)S(1)}, f32[8,4096]{1,0:T(8,128)S(1)}, u32[]{:S(2)}, u32[]{:S(2)}) collective-permute-start(f32[8,4096]{1,0:T(8,128)S(1)} %collective-permute-done.24.refs_2_), channel_id=1, source_target_pairs={{0,1},{1,0},{2,3},{3,2},{4,5},{5,4},{6,7},{7,6},{8,9},{9,8},{10,11... | collective-permute-start | bytes 393224 | tf_op jit(solution)/shard_map/ppermute | solution.py:315
  93.4 7.1 %collective-permute-start.33 = (f32[10,8,512]{2,1,0:T(8,128)S(1)}, f32[10,8,512]{2,1,0:T(8,128)S(1)}, u32[]{:S(2)}, u32[]{:S(2)}) collective-permute-start(f32[10,8,512]{2,1,0:T(8,128)S(1)} %get-tuple-element.68), channel_id=1, source_target_pairs={{0,2},{2,0},{4,6},{6,4},{8,10},{10,8},{12,14},{14,12},{1,3},{3,1},... | collective-permute-start | bytes 491528 | tf_op jit(solution)/shard_map/ppermute | solution.py:315
  94.0 7.7 %collective-permute-start.34 = (f32[10,8,512]{2,1,0:T(8,128)S(1)}, f32[10,8,512]{2,1,0:T(8,128)S(1)}, u32[]{:S(2)}, u32[]{:S(2)}) collective-permute-start(f32[10,8,512]{2,1,0:T(8,128)S(1)} %get-tuple-element.69), channel_id=1, source_target_pairs={{0,4},{2,6},{4,0},{6,2},{8,12},{10,14},{12,8},{14,10},{1,5},{3,7},... | collective-permute-start | bytes 491528 | tf_op jit(solution)/shard_map/ppermute | solution.py:315
  95.6 16.6 %collective-permute-start.35 = (f32[10,8,512]{2,1,0:T(8,128)S(1)}, f32[10,8,512]{2,1,0:T(8,128)S(1)}, u32[]{:S(2)}, u32[]{:S(2)}) collective-permute-start(f32[10,8,512]{2,1,0:T(8,128)S(1)} %get-tuple-element.70), channel_id=1, source_target_pairs={{0,6},{2,4},{4,2},{6,0},{8,14},{10,12},{12,10},{14,8},{1,7},{3,5},... | collective-permute-start | bytes 491528 | tf_op jit(solution)/shard_map/ppermute | solution.py:315
  96.9 15.3 %collective-permute-start.36 = (f32[10,8,512]{2,1,0:T(8,128)S(1)}, f32[10,8,512]{2,1,0:T(8,128)S(1)}, u32[]{:S(2)}, u32[]{:S(2)}) collective-permute-start(f32[10,8,512]{2,1,0:T(8,128)S(1)} %get-tuple-element.71), channel_id=1, source_target_pairs={{0,8},{2,10},{4,12},{6,14},{8,0},{10,2},{12,4},{14,6},{1,9},{3,11}... | collective-permute-start | bytes 491528 | tf_op jit(solution)/shard_map/ppermute | solution.py:315
  98.0 14.3 %collective-permute-start.37 = (f32[10,8,512]{2,1,0:T(8,128)S(1)}, f32[10,8,512]{2,1,0:T(8,128)S(1)}, u32[]{:S(2)}, u32[]{:S(2)}) collective-permute-start(f32[10,8,512]{2,1,0:T(8,128)S(1)} %get-tuple-element.72), channel_id=1, source_target_pairs={{0,10},{2,8},{4,14},{6,12},{8,2},{10,0},{12,6},{14,4},{1,11},{3,9}... | collective-permute-start | bytes 491528 | tf_op jit(solution)/shard_map/ppermute | solution.py:315
  100.5 11.7 %collective-permute-start.38 = (f32[10,8,512]{2,1,0:T(8,128)S(1)}, f32[10,8,512]{2,1,0:T(8,128)S(1)}, u32[]{:S(2)}, u32[]{:S(2)}) collective-permute-start(f32[10,8,512]{2,1,0:T(8,128)S(1)} %get-tuple-element.73), channel_id=1, source_target_pairs={{0,12},{2,14},{4,8},{6,10},{8,4},{10,6},{12,0},{14,2},{1,13},{3,15... | collective-permute-start | bytes 491528 | tf_op jit(solution)/shard_map/ppermute | solution.py:315
  101.7 12.3 %collective-permute-start.39 = (f32[10,8,512]{2,1,0:T(8,128)S(1)}, f32[10,8,512]{2,1,0:T(8,128)S(1)}, u32[]{:S(2)}, u32[]{:S(2)}) collective-permute-start(f32[10,8,512]{2,1,0:T(8,128)S(1)} %get-tuple-element.74), channel_id=1, source_target_pairs={{0,14},{2,12},{4,10},{6,8},{8,6},{10,4},{12,2},{14,0},{1,15},{3,13... | collective-permute-start | bytes 491528 | tf_op jit(solution)/shard_map/ppermute | solution.py:315

commit v2 on v1

--- a/solution.py
+++ b/solution.py
@@ -18,7 +18,7 @@
 
 def plane_order(x_count):
     steps = [(du, dv, dx) for du in range(2) for dv in range(2) for dx in range(x_count)]
-    return sorted(steps[1:], key=lambda step: -sum(part > 0 for part in step))
+    return sorted(steps[1:], key=lambda step: sum(part > 0 for part in step))
 
 
 NT = (((1,), (1,)), ((), ()))
@@ -160,7 +160,7 @@
     lax.fori_loop(0, tiles.shape[0], convert, 0)
 
 
-def product_kernel(x_count, row_local, place, tile_hi, tile_lo, *refs):
+def product_kernel(x_count, row_local, place, tile_hi, tile_lo, after, *refs):
     routed, sides, total = refs[:-5], refs[-5:-1], refs[-1]
     blocks, samples, block = total.shape
     total[...] = jnp.zeros_like(total)
@@ -362,7 +362,7 @@
             chip(loadings.shape, bf16),
         ],
         [(samples, hbm), (loadings, hbm)],
-        [pltpu.SemaphoreType.DMA((5,))],
+        [pltpu.SemaphoreType.DMA((9,))],
     )
     score_terms = lax.all_to_all(score_copies, ROWS, 0, 0, tiled=True)
     row_local, is_diag, slot_index = call(
@@ -389,11 +389,17 @@
         parts = [whole]
         for dx in range(1, x_count):
             parts.append(shift_x(whole, dx))
-        return parts + [swap_core(part) for part in parts]
+        return parts
+
+    def both_cores(parts):
+        swapped = []
+        for part in parts:
+            swapped.append(swap_core(part))
+        return parts + swapped
 
     def exchange(part, dz):
         held = [None] * a_count
-        for da in reversed(range(a_count)):
+        for da in range(a_count):
             held[da] = permute(
                 part,
                 ("a", "u", "v", "k"),
@@ -422,6 +428,7 @@
     resid_parts = own_rows(residual)
     resid_slots = gather_slots(exchange(resid_near, 0), exchange(resid_far, 1), resid_parts)
     routed_resid = deliver(resid_slots)
+    resid_parts = both_cores(resid_parts)
     tiles_hi, tiles_lo = call(
         tile_kernel,
         [chip(tile_shape, bf16), chip(tile_shape, bf16)],
@@ -444,6 +451,7 @@
             (place, smem),
             (tiles_hi, vmem),
             (tiles_lo, vmem),
+            (resid_left, vmem),
         ]
         + [(part, vmem) for part in routed_resid],
         [pltpu.VMEM((blocks_dev, sample_all, block_size), f32)],
@@ -464,6 +472,7 @@
     applied_parts = own_rows(halves[1])
     applied_slots = gather_slots(*exchanged, applied_parts)
     routed_applied = deliver(applied_slots)
+    applied_parts = both_cores(applied_parts)
     partial, new_diagonal = call(
         functools.partial(first_kernel, x_count, scale),
         [chip(tile_shape), (shape(1, var_dev), vmem)],

time: 119 us -> 116 us (0.975)
  starting transfers between devices: 44.7 us -> 42.2 us
    ppermute x40, starting transfers between devices: 37.3 us -> 34.9 us  [permute(): lax.ppermute(value, names, [(at, flat(target(*coords_of(at)))) for at in...]
  transfers between devices with their start and end apart: 41 -> 41, of which waited for: 17 -> 18; matrix products, arithmetic and copies ran while one was open for 0% -> 0% of each run, Pallas kernels for 13% -> 16%
where the time goes in v2:
time: 116 us; the launch traced here: 115 us
  starting transfers between devices  42.2 us (36%)
  waiting for transfers between devices  38.4 us (33%)
  Pallas kernels  32.4 us (28%)
  local copies, waits for them, and re-layouts  1.45 us (1%)
    ppermute x40, waiting for transfers between devices, permute(): lax.ppermute(value, names, [(at, flat(target(*coords_of(at)))) for at in...  35.6 us
    ppermute x40, starting transfers between devices, permute(): lax.ppermute(value, names, [(at, flat(target(*coords_of(at)))) for at in...  34.9 us
    pallas_call x12, Pallas kernels, call(): pl.pallas_call(kernel, out_shape=[out for out, _ in outs], in_specs=specs...  32.4 us
    all_to_all x1, starting transfers between devices, per_device(): score_terms = lax.all_to_all(score_copies, ROWS, 0, 0, tiled=True)  7.32 us
    all_to_all x1, waiting for transfers between devices, per_device(): score_terms = lax.all_to_all(score_copies, ROWS, 0, 0, tiled=True)  2.73 us
  transfers between devices with their start and end apart: 41, of which 18 were waited for; matrix products, arithmetic and copies ran while one was open for 0% of the time, Pallas kernels for 16%

profile of v2, /device:TPU:0, one launch (start us, length us, event | category | flops | bytes accessed | tf_op | source)
XLA Modules:
  0.0 115.3 jit_solution(13227690174870404026)
XLA Ops:
  0.6 3.3 %shard_map.77 = (f32[8,16,256]{2,1,0:T(8,128)}, f32[16,4096]{1,0:T(8,128)S(1)}, bf16[256,4096]{1,0:T(8,128)(2,1)S(1)}) custom-call(f32[16,4096]{1,0:T(8,128)} %samples.1, bf16[256,4096]{1,0:T(8,128)(2,1)} %loadings.1), custom_call_target="tpu_custom_call" | custom-call | tf_op jit(solution)/shard_map/pallas_call | solution.py:334
  3.9 7.3 %all-to-all-start = ((f32[8,16,256]{2,1,0:T(8,128)}), f32[8,16,256]{2,1,0:T(8,128)S(1)}, u32[]{:S(2)}, u32[]{:S(2)}) async-start(f32[8,16,256]{2,1,0:T(8,128)} %get-tuple-element.39.after), calls=%async_computation | async-start | bytes 262144 | tf_op jit(solution)/shard_map/all_to_all | solution.py:367
  11.2 0.1 stack.23.place
  11.3 0.7 copy-done.1
  12.0 0.7 copy-done.2
  12.7 3.2 %shard_map.78 = (s32[10]{0:T(128)S(1)}, s32[10]{0:T(128)S(1)}, s32[80]{0:T(128)S(1)}) custom-call(s32[5]{0:T(128)S(1)} %stack.23.place, s32[320]{0:T(512)S(1)} %copy-done.1, s32[320]{0:T(512)S(1)} %copy-done.2, f32[8,16,256]{2,1,0:T(8,128)} %get-tuple-element.39.after), custom_call_target="tpu_custom_call" | custom-call | tf_op jit(solution)/shard_map/pallas_call | solution.py:334
  15.9 2.7 %all-to-all-done.scores = f32[8,16,256]{2,1,0:T(8,128)S(1)} async-done(((f32[8,16,256]{2,1,0:T(8,128)}), f32[8,16,256]{2,1,0:T(8,128)S(1)}, u32[]{:S(2)}, u32[]{:S(2)}) %all-to-all-start) | async-done | bytes 131104 | tf_op jit(solution)/shard_map/all_to_all | solution.py:367
  18.6 1.0 shard_map.79
  19.6 0.5 collective-permute-start.4
  20.0 1.5 %collective-permute-start.8 = (f32[16,4096]{1,0:T(8,128)S(1)}, f32[16,4096]{1,0:T(8,128)S(1)}, u32[]{:S(2)}, u32[]{:S(2)}) collective-permute-start(f32[16,4096]{1,0:T(8,128)S(1)} %get-tuple-element.47.refs_8_.refs_0_.refs_2_), channel_id=1, source_target_pairs={{0,2},{2,0},{1,3},{3,1},{4,6},{6,4},{5,7},{7,5},{8,10},{10,8},{9,1... | collective-permute-start | bytes 786440 | tf_op jit(solution)/shard_map/ppermute | solution.py:315
  21.5 0.7 collective-permute-start
  22.2 1.9 %collective-permute-start.6 = (f32[8,4096]{1,0:T(8,128)S(1)}, f32[8,4096]{1,0:T(8,128)S(1)}, u32[]{:S(2)}, u32[]{:S(2)}) collective-permute-start(f32[8,4096]{1,0:T(8,128)S(1)} %get-tuple-element.46), channel_id=1, source_target_pairs={{0,24},{1,28},{4,25},{5,29},{8,16},{9,20},{12,17},{13,21},{16,8},{... | collective-permute-start | bytes 393224 | tf_op jit(solution)/shard_map/ppermute | solution.py:315
  24.1 1.3 %collective-permute-start.2 = (f32[8,4096]{1,0:T(8,128)S(1)}, f32[8,4096]{1,0:T(8,128)S(1)}, u32[]{:S(2)}, u32[]{:S(2)}) collective-permute-start(f32[8,4096]{1,0:T(8,128)S(1)} %get-tuple-element.46), channel_id=1, source_target_pairs={{0,8},{1,12},{4,9},{5,13},{8,0},{9,4},{12,1},{13,5},{16,24},{17,28... | collective-permute-start | bytes 393224 | tf_op jit(solution)/shard_map/ppermute | solution.py:315
  25.3 5.8 %collective-permute-done.4.refs_4_ = f32[8,4096]{1,0:T(8,128)S(1)} collective-permute-done((f32[8,4096]{1,0:T(8,128)S(1)}, f32[8,4096]{1,0:T(8,128)S(1)}, u32[]{:S(2)}, u32[]{:S(2)}) %collective-permute-start.4) | collective-permute-done | bytes 131104 | tf_op jit(solution)/shard_map/ppermute | solution.py:315
  31.1 0.5 collective-permute-start.1
  31.7 0.1 collective-permute-start.7
  31.7 2.6 %collective-permute-done.2.refs_2_ = f32[8,4096]{1,0:T(8,128)S(1)} collective-permute-done((f32[8,4096]{1,0:T(8,128)S(1)}, f32[8,4096]{1,0:T(8,128)S(1)}, u32[]{:S(2)}, u32[]{:S(2)}) %collective-permute-start.2) | collective-permute-done | bytes 131104 | tf_op jit(solution)/shard_map/ppermute | solution.py:315
  34.3 0.5 collective-permute-start.9
  34.8 0.1 collective-permute-start.10
  34.9 0.8 collective-permute-done.3.refs_3_
  35.7 1.1 shard_map.80
  36.8 1.6 %collective-permute-start.11 = (f32[10,8,512]{2,1,0:T(8,128)S(1)}, f32[10,8,512]{2,1,0:T(8,128)S(1)}, u32[]{:S(2)}, u32[]{:S(2)}) collective-permute-start(f32[10,8,512]{2,1,0:T(8,128)S(1)} %get-tuple-element.53), channel_id=1, source_target_pairs={{0,2},{2,0},{4,6},{6,4},{8,10},{10,8},{12,14},{14,12},{1,3},{3,1},... | collective-permute-start | bytes 491528 | tf_op jit(solution)/shard_map/ppermute | solution.py:315
  38.3 1.6 %collective-permute-start.12 = (f32[10,8,512]{2,1,0:T(8,128)S(1)}, f32[10,8,512]{2,1,0:T(8,128)S(1)}, u32[]{:S(2)}, u32[]{:S(2)}) collective-permute-start(f32[10,8,512]{2,1,0:T(8,128)S(1)} %get-tuple-element.54), channel_id=1, source_target_pairs={{0,4},{2,6},{4,0},{6,2},{8,12},{10,14},{12,8},{14,10},{1,5},{3,7},... | collective-permute-start | bytes 491528 | tf_op jit(solution)/shard_map/ppermute | solution.py:315
  39.9 0.4 collective-permute-start.13
  40.3 0.9 collective-permute-start.14
  41.2 2.7 %collective-permute-done.11.refs_1_.refs_5_ = f32[10,8,512]{2,1,0:T(8,128)S(1)} collective-permute-done((f32[10,8,512]{2,1,0:T(8,128)S(1)}, f32[10,8,512]{2,1,0:T(8,128)S(1)}, u32[]{:S(2)}, u32[]{:S(2)}) %collective-permute-start.11) | collective-permute-done | bytes 163872 | tf_op jit(solution)/shard_map/ppermute | solution.py:315
  43.9 1.8 %collective-permute-start.15 = (f32[10,8,512]{2,1,0:T(8,128)S(1)}, f32[10,8,512]{2,1,0:T(8,128)S(1)}, u32[]{:S(2)}, u32[]{:S(2)}) collective-permute-start(f32[10,8,512]{2,1,0:T(8,128)S(1)} %get-tuple-element.57), channel_id=1, source_target_pairs={{0,10},{2,8},{4,14},{6,12},{8,2},{10,0},{12,6},{14,4},{1,11},{3,9}... | collective-permute-start | bytes 491528 | tf_op jit(solution)/shard_map/ppermute | solution.py:315
  45.7 1.5 %collective-permute-done.12.refs_2_.refs_6_ = f32[10,8,512]{2,1,0:T(8,128)S(1)} collective-permute-done((f32[10,8,512]{2,1,0:T(8,128)S(1)}, f32[10,8,512]{2,1,0:T(8,128)S(1)}, u32[]{:S(2)}, u32[]{:S(2)}) %collective-permute-start.12) | collective-permute-done | bytes 163872 | tf_op jit(solution)/shard_map/ppermute | solution.py:315
  47.2 2.3 %collective-permute-start.16 = (f32[10,8,512]{2,1,0:T(8,128)S(1)}, f32[10,8,512]{2,1,0:T(8,128)S(1)}, u32[]{:S(2)}, u32[]{:S(2)}) collective-permute-start(f32[10,8,512]{2,1,0:T(8,128)S(1)} %get-tuple-element.58), channel_id=1, source_target_pairs={{0,12},{2,14},{4,8},{6,10},{8,4},{10,6},{12,0},{14,2},{1,13},{3,15... | collective-permute-start | bytes 491528 | tf_op jit(solution)/shard_map/ppermute | solution.py:315
  49.5 4.8 %shard_map.82 = (bf16[10,512,512]{2,1,0:T(8,128)(2,1)S(1)}, bf16[10,512,512]{2,1,0:T(8,128)(2,1)S(1)}) custom-call(s32[10]{0:T(128)S(1)} %get-tuple-element.41.is_diag, f32[10,512,512]{2,1,0:T(8,128)} %tiles.3, f32[10,8,512]{2,1,0:T(8,128)S(1)} %get-tuple-element.48.after.refs_0_.refs_4_), custom_call_target="tpu_custom_call" | custom-call | bytes 20971520 | tf_op jit(solution)/shard_map/pallas_call | solution.py:334
  54.3 1.5 %shard_map.81 = (f32[64,4096]{1,0:T(8,128)S(1)}, bf16[8,512,192]{2,1,0:T(8,128)(2,1)S(1)}) custom-call(s32[5]{0:T(128)S(1)} %stack.23.place, f32[10,8,512]{2,1,0:T(8,128)S(1)} %get-tuple-element.48.after.refs_0_.refs_4_, f32[16,4096]{1,0:T(8,128)S(1)} %get-tuple-element.47.refs_8_.refs_0_.refs_2_, f32[16,4096]{1,0:T(8,128)S(1)} %collective-permute-done.8.refs_9_.refs_1_, ...), custom_call_target="tpu_custom_call" | custom-call | bytes 4194304 | tf_op jit(solution)/shard_map/pallas_call | solution.py:334
  55.8 0.3 collective-permute-done.16.refs_6_.refs_10_
  56.1 2.1 %collective-permute-done.17.refs_7_.refs_11_ = f32[10,8,512]{2,1,0:T(8,128)S(1)} collective-permute-done((f32[10,8,512]{2,1,0:T(8,128)S(1)}, f32[10,8,512]{2,1,0:T(8,128)S(1)}, u32[]{:S(2)}, u32[]{:S(2)}) %collective-permute-start.17) | collective-permute-done | bytes 163872 | tf_op jit(solution)/shard_map/ppermute | solution.py:315
  58.2 5.2 %shard_map.83 = (f32[2,8,4096]{2,1,0:T(8,128)S(1)}, f32[2,8,4096]{2,1,0:T(8,128)S(1)}, f32[2,8,4096]{2,1,0:T(8,128)S(1)}, f32[2,8,4096]{2,1,0:T(8,128)S(1)}) custom-call(s32[10]{0:T(128)S(1)} %get-tuple-element.40.row_local, s32[5]{0:T(128)S(1)} %stack.23.place, bf16[10,512,512]{2,1,0:T(8,128)(2,1)S(1)} %get-tuple-element.51.tile_hi, ...), custom_call_target="tpu_custom_call" | custom-call | tf_op jit(solution)/shard_map/pallas_call | solution.py:334
  63.5 0.1 collective-permute-start.18
  63.5 0.5 collective-permute-start.22
  64.0 1.0 collective-permute-done.18.refs_1_
  65.1 0.8 collective-permute-start.19
  65.9 1.4 %collective-permute-start.23 = (f32[8,4096]{1,0:T(8,128)S(1)}, f32[8,4096]{1,0:T(8,128)S(1)}, u32[]{:S(2)}, u32[]{:S(2)}) collective-permute-start(f32[8,4096]{1,0:T(8,128)S(1)} %fusion), channel_id=1, source_target_pairs={{0,2},{2,0},{1,3},{3,1},{4,6},{6,4},{5,7},{7,5},{8,10},{10,8},{9,1... | collective-permute-start | bytes 393224 | tf_op jit(solution)/shard_map/ppermute | solution.py:315
  67.3 4.3 %collective-permute-done.19.refs_4_ = f32[8,4096]{1,0:T(8,128)S(1)} collective-permute-done((f32[8,4096]{1,0:T(8,128)S(1)}, f32[8,4096]{1,0:T(8,128)S(1)}, u32[]{:S(2)}, u32[]{:S(2)}) %collective-permute-start.19) | collective-permute-done | bytes 131104 | tf_op jit(solution)/shard_map/ppermute | solution.py:315
  71.6 1.6 %collective-permute-start.26 = (f32[8,4096]{1,0:T(8,128)S(1)}, f32[8,4096]{1,0:T(8,128)S(1)}, u32[]{:S(2)}, u32[]{:S(2)}) collective-permute-start(f32[8,4096]{1,0:T(8,128)S(1)} %shard_map.84.refs_5_), channel_id=1, source_target_pairs={{0,16},{1,20},{4,17},{5,21},{8,24},{9,28},{12,25},{13,29},{16,0},{... | collective-permute-start | bytes 393224 | tf_op jit(solution)/shard_map/ppermute | solution.py:315
  73.2 0.3 collective-permute-done.23.refs_4_
  73.6 0.9 collective-permute-start.30
  74.4 0.7 collective-permute-start.20
  75.1 2.7 %collective-permute-start.28 = (f32[8,4096]{1,0:T(8,128)S(1)}, f32[8,4096]{1,0:T(8,128)S(1)}, u32[]{:S(2)}, u32[]{:S(2)}) collective-permute-start(f32[8,4096]{1,0:T(8,128)S(1)} %get-tuple-element.64), channel_id=1, source_target_pairs={{0,24},{1,28},{4,25},{5,29},{8,16},{9,20},{12,17},{13,21},{16,8},{... | collective-permute-start | bytes 393224 | tf_op jit(solution)/shard_map/ppermute | solution.py:315
  77.8 5.8 %collective-permute-done.26.refs_4_ = f32[8,4096]{1,0:T(8,128)S(1)} collective-permute-done((f32[8,4096]{1,0:T(8,128)S(1)}, f32[8,4096]{1,0:T(8,128)S(1)}, u32[]{:S(2)}, u32[]{:S(2)}) %collective-permute-start.26) | collective-permute-done | bytes 131104 | tf_op jit(solution)/shard_map/ppermute | solution.py:315
  83.6 0.5 collective-permute-start.21
  84.1 0.8 collective-permute-start.29
  84.8 1.7 %collective-permute-done.24.refs_2_ = f32[8,4096]{1,0:T(8,128)S(1)} collective-permute-done((f32[8,4096]{1,0:T(8,128)S(1)}, f32[8,4096]{1,0:T(8,128)S(1)}, u32[]{:S(2)}, u32[]{:S(2)}) %collective-permute-start.24) | collective-permute-done | bytes 131104 | tf_op jit(solution)/shard_map/ppermute | solution.py:315
  86.5 0.5 collective-permute-start.31
  87.1 0.8 collective-permute-done.25.refs_3_
  87.9 1.1 shard_map.86
  89.0 1.5 %collective-permute-start.33 = (f32[10,8,512]{2,1,0:T(8,128)S(1)}, f32[10,8,512]{2,1,0:T(8,128)S(1)}, u32[]{:S(2)}, u32[]{:S(2)}) collective-permute-start(f32[10,8,512]{2,1,0:T(8,128)S(1)} %get-tuple-element.68), channel_id=1, source_target_pairs={{0,2},{2,0},{4,6},{6,4},{8,10},{10,8},{12,14},{14,12},{1,3},{3,1},... | collective-permute-start | bytes 491528 | tf_op jit(solution)/shard_map/ppermute | solution.py:315
  90.5 1.6 %collective-permute-start.34 = (f32[10,8,512]{2,1,0:T(8,128)S(1)}, f32[10,8,512]{2,1,0:T(8,128)S(1)}, u32[]{:S(2)}, u32[]{:S(2)}) collective-permute-start(f32[10,8,512]{2,1,0:T(8,128)S(1)} %get-tuple-element.69), channel_id=1, source_target_pairs={{0,4},{2,6},{4,0},{6,2},{8,12},{10,14},{12,8},{14,10},{1,5},{3,7},... | collective-permute-start | bytes 491528 | tf_op jit(solution)/shard_map/ppermute | solution.py:315
  92.1 0.5 collective-permute-start.35
  92.6 1.1 collective-permute-start.36
  93.7 2.5 %collective-permute-done.33.refs_1_ = f32[10,8,512]{2,1,0:T(8,128)S(1)} collective-permute-done((f32[10,8,512]{2,1,0:T(8,128)S(1)}, f32[10,8,512]{2,1,0:T(8,128)S(1)}, u32[]{:S(2)}, u32[]{:S(2)}) %collective-permute-start.33) | collective-permute-done | bytes 163872 | tf_op jit(solution)/shard_map/ppermute | solution.py:315
  96.2 1.7 %collective-permute-start.37 = (f32[10,8,512]{2,1,0:T(8,128)S(1)}, f32[10,8,512]{2,1,0:T(8,128)S(1)}, u32[]{:S(2)}, u32[]{:S(2)}) collective-permute-start(f32[10,8,512]{2,1,0:T(8,128)S(1)} %get-tuple-element.72), channel_id=1, source_target_pairs={{0,10},{2,8},{4,14},{6,12},{8,2},{10,0},{12,6},{14,4},{1,11},{3,9}... | collective-permute-start | bytes 491528 | tf_op jit(solution)/shard_map/ppermute | solution.py:315
  97.8 1.3 %collective-permute-done.34.refs_2_ = f32[10,8,512]{2,1,0:T(8,128)S(1)} collective-permute-done((f32[10,8,512]{2,1,0:T(8,128)S(1)}, f32[10,8,512]{2,1,0:T(8,128)S(1)}, u32[]{:S(2)}, u32[]{:S(2)}) %collective-permute-start.34) | collective-permute-done | bytes 163872 | tf_op jit(solution)/shard_map/ppermute | solution.py:315
  99.1 2.7 %collective-permute-start.38 = (f32[10,8,512]{2,1,0:T(8,128)S(1)}, f32[10,8,512]{2,1,0:T(8,128)S(1)}, u32[]{:S(2)}, u32[]{:S(2)}) collective-permute-start(f32[10,8,512]{2,1,0:T(8,128)S(1)} %get-tuple-element.73), channel_id=1, source_target_pairs={{0,12},{2,14},{4,8},{6,10},{8,4},{10,6},{12,0},{14,2},{1,13},{3,15... | collective-permute-start | bytes 491528 | tf_op jit(solution)/shard_map/ppermute | solution.py:315
  101.8 6.3 %shard_map.87 = (f32[10,512,512]{2,1,0:T(8,128)S(1)}, f32[1,4096]{1,0:T(1,128)}) custom-call(s32[10]{0:T(128)S(1)} %get-tuple-element.40.row_local, s32[5]{0:T(128)S(1)} %stack.23.place, f32[10,512,512]{2,1,0:T(8,128)} %tiles.3, f32[1,4096]{1,0:T(1,128)S(1)} %bitcast.13, f32[64,4096]{1,0:T(8,128)S(1)} %get-tuple-element.50.resid_rows, ...), custom_call_target="tpu_custom_call" | custom-call | flops 1006632960 | bytes 41943040 | tf_op jit(solution)/shard_map/pallas_call | solution.py:334
  108.1 0.2 collective-permute-done.38.refs_6_
  108.3 2.1 %collective-permute-done.39.refs_7_ = f32[10,8,512]{2,1,0:T(8,128)S(1)} collective-permute-done((f32[10,8,512]{2,1,0:T(8,128)S(1)}, f32[10,8,512]{2,1,0:T(8,128)S(1)}, u32[]{:S(2)}, u32[]{:S(2)}) %collective-permute-start.39) | collective-permute-done | bytes 163872 | tf_op jit(solution)/shard_map/ppermute | solution.py:315
  110.4 4.9 %shard_map.88 = f32[10,512,512]{2,1,0:T(8,128)} custom-call(s32[10]{0:T(128)S(1)} %get-tuple-element.40.row_local, s32[10]{0:T(128)S(1)} %get-tuple-element.41.is_diag, bf16[8,512,192]{2,1,0:T(8,128)(2,1)S(1)} %get-tuple-element.49.after.left, f32[10,512,512]{2,1,0:T(8,128)S(1)} %get-tuple-element.67.partial, ...), custom_call_target="tpu_custom_call" | custom-call | tf_op jit(solution)/shard_map/pallas_call | solution.py:334
  (39 shorter events, 0.3 us)
Async XLA Ops:
  3.9 14.7 %all-to-all-start = ((f32[8,16,256]{2,1,0:T(8,128)}), f32[8,16,256]{2,1,0:T(8,128)S(1)}, u32[]{:S(2)}, u32[]{:S(2)}) async-start(f32[8,16,256]{2,1,0:T(8,128)} %get-tuple-element.39.after), calls=%async_computation | async-start | bytes 262144 | tf_op jit(solution)/shard_map/all_to_all | solution.py:367
  11.3 0.7 copy-start.1
  12.0 0.7 copy-start.2
  19.6 11.6 %collective-permute-start.4 = (f32[8,4096]{1,0:T(8,128)S(1)}, f32[8,4096]{1,0:T(8,128)S(1)}, u32[]{:S(2)}, u32[]{:S(2)}) collective-permute-start(f32[8,4096]{1,0:T(8,128)S(1)} %get-tuple-element.45), channel_id=1, source_target_pairs={{0,16},{1,20},{4,17},{5,21},{8,24},{9,28},{12,25},{13,29},{16,0},{... | collective-permute-start | bytes 393224 | tf_op jit(solution)/shard_map/ppermute | solution.py:315
  20.0 14.8 %collective-permute-start.8 = (f32[16,4096]{1,0:T(8,128)S(1)}, f32[16,4096]{1,0:T(8,128)S(1)}, u32[]{:S(2)}, u32[]{:S(2)}) collective-permute-start(f32[16,4096]{1,0:T(8,128)S(1)} %get-tuple-element.47.refs_8_.refs_0_.refs_2_), channel_id=1, source_target_pairs={{0,2},{2,0},{1,3},{3,1},{4,6},{6,4},{5,7},{7,5},{8,10},{10,8},{9,1... | collective-permute-start | bytes 786440 | tf_op jit(solution)/shard_map/ppermute | solution.py:315
  21.5 9.6 %collective-permute-start = (f32[8,4096]{1,0:T(8,128)S(1)}, f32[8,4096]{1,0:T(8,128)S(1)}, u32[]{:S(2)}, u32[]{:S(2)}) collective-permute-start(f32[8,4096]{1,0:T(8,128)S(1)} %get-tuple-element.45), channel_id=1, source_target_pairs={{0,0},{1,4},{4,1},{5,5},{8,8},{9,12},{12,9},{13,13},{16,16},{17,20... | collective-permute-start | bytes 393224 | tf_op jit(solution)/shard_map/ppermute | solution.py:315
  22.2 9.5 %collective-permute-start.6 = (f32[8,4096]{1,0:T(8,128)S(1)}, f32[8,4096]{1,0:T(8,128)S(1)}, u32[]{:S(2)}, u32[]{:S(2)}) collective-permute-start(f32[8,4096]{1,0:T(8,128)S(1)} %get-tuple-element.46), channel_id=1, source_target_pairs={{0,24},{1,28},{4,25},{5,29},{8,16},{9,20},{12,17},{13,21},{16,8},{... | collective-permute-start | bytes 393224 | tf_op jit(solution)/shard_map/ppermute | solution.py:315
  24.1 10.2 %collective-permute-start.2 = (f32[8,4096]{1,0:T(8,128)S(1)}, f32[8,4096]{1,0:T(8,128)S(1)}, u32[]{:S(2)}, u32[]{:S(2)}) collective-permute-start(f32[8,4096]{1,0:T(8,128)S(1)} %get-tuple-element.46), channel_id=1, source_target_pairs={{0,8},{1,12},{4,9},{5,13},{8,0},{9,4},{12,1},{13,5},{16,24},{17,28... | collective-permute-start | bytes 393224 | tf_op jit(solution)/shard_map/ppermute | solution.py:315
  31.1 3.2 %collective-permute-start.5 = (f32[8,4096]{1,0:T(8,128)S(1)}, f32[8,4096]{1,0:T(8,128)S(1)}, u32[]{:S(2)}, u32[]{:S(2)}) collective-permute-start(f32[8,4096]{1,0:T(8,128)S(1)} %collective-permute-done.4.refs_4_), channel_id=1, source_target_pairs={{0,1},{1,0},{2,3},{3,2},{4,5},{5,4},{6,7},{7,6},{8,9},{9,8},{10,11... | collective-permute-start | bytes 393224 | tf_op jit(solution)/shard_map/ppermute | solution.py:315
  31.1 3.8 %collective-permute-start.1 = (f32[8,4096]{1,0:T(8,128)S(1)}, f32[8,4096]{1,0:T(8,128)S(1)}, u32[]{:S(2)}, u32[]{:S(2)}) collective-permute-start(f32[8,4096]{1,0:T(8,128)S(1)} %collective-permute-done.refs_0_), channel_id=1, source_target_pairs={{0,1},{1,0},{2,3},{3,2},{4,5},{5,4},{6,7},{7,6},{8,9},{9,8},{10,11... | collective-permute-start | bytes 393224 | tf_op jit(solution)/shard_map/ppermute | solution.py:315
  31.7 3.2 %collective-permute-start.7 = (f32[8,4096]{1,0:T(8,128)S(1)}, f32[8,4096]{1,0:T(8,128)S(1)}, u32[]{:S(2)}, u32[]{:S(2)}) collective-permute-start(f32[8,4096]{1,0:T(8,128)S(1)} %collective-permute-done.6.refs_6_), channel_id=1, source_target_pairs={{0,1},{1,0},{2,3},{3,2},{4,5},{5,4},{6,7},{7,6},{8,9},{9,8},{10,11... | collective-permute-start | bytes 393224 | tf_op jit(solution)/shard_map/ppermute | solution.py:315
  34.3 1.3 %collective-permute-start.3 = (f32[8,4096]{1,0:T(8,128)S(1)}, f32[8,4096]{1,0:T(8,128)S(1)}, u32[]{:S(2)}, u32[]{:S(2)}) collective-permute-start(f32[8,4096]{1,0:T(8,128)S(1)} %collective-permute-done.2.refs_2_), channel_id=1, source_target_pairs={{0,1},{1,0},{2,3},{3,2},{4,5},{5,4},{6,7},{7,6},{8,9},{9,8},{10,11... | collective-permute-start | bytes 393224 | tf_op jit(solution)/shard_map/ppermute | solution.py:315
  34.3 6.0 %collective-permute-start.9 = (f32[16,4096]{1,0:T(8,128)S(1)}, f32[16,4096]{1,0:T(8,128)S(1)}, u32[]{:S(2)}, u32[]{:S(2)}) collective-permute-start(f32[16,4096]{1,0:T(8,128)S(1)} %get-tuple-element.47.refs_8_.refs_0_.refs_2_), channel_id=1, source_target_pairs={{0,1},{1,0},{2,3},{3,2},{4,5},{5,4},{6,7},{7,6},{8,9},{9,8},{10,11... | collective-permute-start | bytes 786440 | tf_op jit(solution)/shard_map/ppermute | solution.py:315
  34.8 14.7 %collective-permute-start.10 = (f32[16,4096]{1,0:T(8,128)S(1)}, f32[16,4096]{1,0:T(8,128)S(1)}, u32[]{:S(2)}, u32[]{:S(2)}) collective-permute-start(f32[16,4096]{1,0:T(8,128)S(1)} %collective-permute-done.8.refs_9_.refs_1_), channel_id=1, source_target_pairs={{0,1},{1,0},{2,3},{3,2},{4,5},{5,4},{6,7},{7,6},{8,9},{9,8},{10,11... | collective-permute-start | bytes 786440 | tf_op jit(solution)/shard_map/ppermute | solution.py:315
  36.8 7.1 %collective-permute-start.11 = (f32[10,8,512]{2,1,0:T(8,128)S(1)}, f32[10,8,512]{2,1,0:T(8,128)S(1)}, u32[]{:S(2)}, u32[]{:S(2)}) collective-permute-start(f32[10,8,512]{2,1,0:T(8,128)S(1)} %get-tuple-element.53), channel_id=1, source_target_pairs={{0,2},{2,0},{4,6},{6,4},{8,10},{10,8},{12,14},{14,12},{1,3},{3,1},... | collective-permute-start | bytes 491528 | tf_op jit(solution)/shard_map/ppermute | solution.py:315
  38.3 8.9 %collective-permute-start.12 = (f32[10,8,512]{2,1,0:T(8,128)S(1)}, f32[10,8,512]{2,1,0:T(8,128)S(1)}, u32[]{:S(2)}, u32[]{:S(2)}) collective-permute-start(f32[10,8,512]{2,1,0:T(8,128)S(1)} %get-tuple-element.54), channel_id=1, source_target_pairs={{0,4},{2,6},{4,0},{6,2},{8,12},{10,14},{12,8},{14,10},{1,5},{3,7},... | collective-permute-start | bytes 491528 | tf_op jit(solution)/shard_map/ppermute | solution.py:315
  39.9 15.9 %collective-permute-start.13 = (f32[10,8,512]{2,1,0:T(8,128)S(1)}, f32[10,8,512]{2,1,0:T(8,128)S(1)}, u32[]{:S(2)}, u32[]{:S(2)}) collective-permute-start(f32[10,8,512]{2,1,0:T(8,128)S(1)} %get-tuple-element.55), channel_id=1, source_target_pairs={{0,6},{2,4},{4,2},{6,0},{8,14},{10,12},{12,10},{14,8},{1,7},{3,5},... | collective-permute-start | bytes 491528 | tf_op jit(solution)/shard_map/ppermute | solution.py:315
  40.3 15.5 %collective-permute-start.14 = (f32[10,8,512]{2,1,0:T(8,128)S(1)}, f32[10,8,512]{2,1,0:T(8,128)S(1)}, u32[]{:S(2)}, u32[]{:S(2)}) collective-permute-start(f32[10,8,512]{2,1,0:T(8,128)S(1)} %get-tuple-element.56), channel_id=1, source_target_pairs={{0,8},{2,10},{4,12},{6,14},{8,0},{10,2},{12,4},{14,6},{1,9},{3,11}... | collective-permute-start | bytes 491528 | tf_op jit(solution)/shard_map/ppermute | solution.py:315
  43.9 11.9 %collective-permute-start.15 = (f32[10,8,512]{2,1,0:T(8,128)S(1)}, f32[10,8,512]{2,1,0:T(8,128)S(1)}, u32[]{:S(2)}, u32[]{:S(2)}) collective-permute-start(f32[10,8,512]{2,1,0:T(8,128)S(1)} %get-tuple-element.57), channel_id=1, source_target_pairs={{0,10},{2,8},{4,14},{6,12},{8,2},{10,0},{12,6},{14,4},{1,11},{3,9}... | collective-permute-start | bytes 491528 | tf_op jit(solution)/shard_map/ppermute | solution.py:315
  47.2 8.9 %collective-permute-start.16 = (f32[10,8,512]{2,1,0:T(8,128)S(1)}, f32[10,8,512]{2,1,0:T(8,128)S(1)}, u32[]{:S(2)}, u32[]{:S(2)}) collective-permute-start(f32[10,8,512]{2,1,0:T(8,128)S(1)} %get-tuple-element.58), channel_id=1, source_target_pairs={{0,12},{2,14},{4,8},{6,10},{8,4},{10,6},{12,0},{14,2},{1,13},{3,15... | collective-permute-start | bytes 491528 | tf_op jit(solution)/shard_map/ppermute | solution.py:315
  49.5 8.8 %collective-permute-start.17 = (f32[10,8,512]{2,1,0:T(8,128)S(1)}, f32[10,8,512]{2,1,0:T(8,128)S(1)}, u32[]{:S(2)}, u32[]{:S(2)}) collective-permute-start(f32[10,8,512]{2,1,0:T(8,128)S(1)} %get-tuple-element.59), channel_id=1, source_target_pairs={{0,14},{2,12},{4,10},{6,8},{8,6},{10,4},{12,2},{14,0},{1,15},{3,13... | collective-permute-start | bytes 491528 | tf_op jit(solution)/shard_map/ppermute | solution.py:315
  58.2 13.3 %copy-start = (f32[4096]{0:T(1024)S(1)}, f32[4096]{0:T(1024)}, u32[]{:S(2)}) copy-start(f32[4096]{0:T(1024)} %param.9) | copy-start | bytes 49156
  63.5 1.6 %collective-permute-start.18 = (f32[2,8,4096]{2,1,0:T(8,128)S(1)}, f32[2,8,4096]{2,1,0:T(8,128)S(1)}, u32[]{:S(2)}, u32[]{:S(2)}) collective-permute-start(f32[2,8,4096]{2,1,0:T(8,128)S(1)} %get-tuple-element.61), channel_id=1, source_target_pairs={{0,1},{1,0},{2,3},{3,2},{4,5},{5,4},{6,7},{7,6},{8,9},{9,8},{10,11... | collective-permute-start | bytes 786440 | tf_op jit(solution)/shard_map/ppermute | solution.py:315
  63.5 2.3 %collective-permute-start.22 = (f32[2,8,4096]{2,1,0:T(8,128)S(1)}, f32[2,8,4096]{2,1,0:T(8,128)S(1)}, u32[]{:S(2)}, u32[]{:S(2)}) collective-permute-start(f32[2,8,4096]{2,1,0:T(8,128)S(1)} %get-tuple-element.63), channel_id=1, source_target_pairs={{0,1},{1,0},{2,3},{3,2},{4,5},{5,4},{6,7},{7,6},{8,9},{9,8},{10,11... | collective-permute-start | bytes 786440 | tf_op jit(solution)/shard_map/ppermute | solution.py:315
  65.1 6.4 %collective-permute-start.19 = (f32[8,4096]{1,0:T(8,128)S(1)}, f32[8,4096]{1,0:T(8,128)S(1)}, u32[]{:S(2)}, u32[]{:S(2)}) collective-permute-start(f32[8,4096]{1,0:T(8,128)S(1)} %fusion.1), channel_id=1, source_target_pairs={{0,2},{2,0},{1,3},{3,1},{4,6},{6,4},{5,7},{7,5},{8,10},{10,8},{9,1... | collective-permute-start | bytes 393224 | tf_op jit(solution)/shard_map/ppermute | solution.py:315
  65.9 7.6 %collective-permute-start.23 = (f32[8,4096]{1,0:T(8,128)S(1)}, f32[8,4096]{1,0:T(8,128)S(1)}, u32[]{:S(2)}, u32[]{:S(2)}) collective-permute-start(f32[8,4096]{1,0:T(8,128)S(1)} %fusion), channel_id=1, source_target_pairs={{0,2},{2,0},{1,3},{3,1},{4,6},{6,4},{5,7},{7,5},{8,10},{10,8},{9,1... | collective-permute-start | bytes 393224 | tf_op jit(solution)/shard_map/ppermute | solution.py:315
  71.6 12.0 %collective-permute-start.26 = (f32[8,4096]{1,0:T(8,128)S(1)}, f32[8,4096]{1,0:T(8,128)S(1)}, u32[]{:S(2)}, u32[]{:S(2)}) collective-permute-start(f32[8,4096]{1,0:T(8,128)S(1)} %shard_map.84.refs_5_), channel_id=1, source_target_pairs={{0,16},{1,20},{4,17},{5,21},{8,24},{9,28},{12,25},{13,29},{16,0},{... | collective-permute-start | bytes 393224 | tf_op jit(solution)/shard_map/ppermute | solution.py:315
  73.6 13.5 %collective-permute-start.30 = (f32[16,4096]{1,0:T(8,128)S(1)}, f32[16,4096]{1,0:T(8,128)S(1)}, u32[]{:S(2)}, u32[]{:S(2)}) collective-permute-start(f32[16,4096]{1,0:T(8,128)S(1)} %get-tuple-element.65.refs_8_.refs_0_), channel_id=1, source_target_pairs={{0,2},{2,0},{1,3},{3,1},{4,6},{6,4},{5,7},{7,5},{8,10},{10,8},{9,1... | collective-permute-start | bytes 786440 | tf_op jit(solution)/shard_map/ppermute | solution.py:315
  74.4 9.1 %collective-permute-start.20 = (f32[8,4096]{1,0:T(8,128)S(1)}, f32[8,4096]{1,0:T(8,128)S(1)}, u32[]{:S(2)}, u32[]{:S(2)}) collective-permute-start(f32[8,4096]{1,0:T(8,128)S(1)} %shard_map.84.refs_5_), channel_id=1, source_target_pairs={{0,0},{1,4},{4,1},{5,5},{8,8},{9,12},{12,9},{13,13},{16,16},{17,20... | collective-permute-start | bytes 393224 | tf_op jit(solution)/shard_map/ppermute | solution.py:315
  75.1 9.0 %collective-permute-start.28 = (f32[8,4096]{1,0:T(8,128)S(1)}, f32[8,4096]{1,0:T(8,128)S(1)}, u32[]{:S(2)}, u32[]{:S(2)}) collective-permute-start(f32[8,4096]{1,0:T(8,128)S(1)} %get-tuple-element.64), channel_id=1, source_target_pairs={{0,24},{1,28},{4,25},{5,29},{8,16},{9,20},{12,17},{13,21},{16,8},{... | collective-permute-start | bytes 393224 | tf_op jit(solution)/shard_map/ppermute | solution.py:315
  77.8 8.7 %collective-permute-start.24 = (f32[8,4096]{1,0:T(8,128)S(1)}, f32[8,4096]{1,0:T(8,128)S(1)}, u32[]{:S(2)}, u32[]{:S(2)}) collective-permute-start(f32[8,4096]{1,0:T(8,128)S(1)} %get-tuple-element.64), channel_id=1, source_target_pairs={{0,8},{1,12},{4,9},{5,13},{8,0},{9,4},{12,1},{13,5},{16,24},{17,28... | collective-permute-start | bytes 393224 | tf_op jit(solution)/shard_map/ppermute | solution.py:315
  83.6 3.0 %collective-permute-start.27 = (f32[8,4096]{1,0:T(8,128)S(1)}, f32[8,4096]{1,0:T(8,128)S(1)}, u32[]{:S(2)}, u32[]{:S(2)}) collective-permute-start(f32[8,4096]{1,0:T(8,128)S(1)} %collective-permute-done.26.refs_4_), channel_id=1, source_target_pairs={{0,1},{1,0},{2,3},{3,2},{4,5},{5,4},{6,7},{7,6},{8,9},{9,8},{10,11... | collective-permute-start | bytes 393224 | tf_op jit(solution)/shard_map/ppermute | solution.py:315
  83.6 3.6 %collective-permute-start.21 = (f32[8,4096]{1,0:T(8,128)S(1)}, f32[8,4096]{1,0:T(8,128)S(1)}, u32[]{:S(2)}, u32[]{:S(2)}) collective-permute-start(f32[8,4096]{1,0:T(8,128)S(1)} %collective-permute-done.20.refs_0_), channel_id=1, source_target_pairs={{0,1},{1,0},{2,3},{3,2},{4,5},{5,4},{6,7},{7,6},{8,9},{9,8},{10,11... | collective-permute-start | bytes 393224 | tf_op jit(solution)/shard_map/ppermute | solution.py:315
  84.1 3.1 %collective-permute-start.29 = (f32[8,4096]{1,0:T(8,128)S(1)}, f32[8,4096]{1,0:T(8,128)S(1)}, u32[]{:S(2)}, u32[]{:S(2)}) collective-permute-start(f32[8,4096]{1,0:T(8,128)S(1)} %collective-permute-done.28.refs_6_), channel_id=1, source_target_pairs={{0,1},{1,0},{2,3},{3,2},{4,5},{5,4},{6,7},{7,6},{8,9},{9,8},{10,11... | collective-permute-start | bytes 393224 | tf_op jit(solution)/shard_map/ppermute | solution.py:315
  86.5 1.3 %collective-permute-start.25 = (f32[8,4096]{1,0:T(8,128)S(1)}, f32[8,4096]{1,0:T(8,128)S(1)}, u32[]{:S(2)}, u32[]{:S(2)}) collective-permute-start(f32[8,4096]{1,0:T(8,128)S(1)} %collective-permute-done.24.refs_2_), channel_id=1, source_target_pairs={{0,1},{1,0},{2,3},{3,2},{4,5},{5,4},{6,7},{7,6},{8,9},{9,8},{10,11... | collective-permute-start | bytes 393224 | tf_op jit(solution)/shard_map/ppermute | solution.py:315
  86.5 6.0 %collective-permute-start.31 = (f32[16,4096]{1,0:T(8,128)S(1)}, f32[16,4096]{1,0:T(8,128)S(1)}, u32[]{:S(2)}, u32[]{:S(2)}) collective-permute-start(f32[16,4096]{1,0:T(8,128)S(1)} %get-tuple-element.65.refs_8_.refs_0_), channel_id=1, source_target_pairs={{0,1},{1,0},{2,3},{3,2},{4,5},{5,4},{6,7},{7,6},{8,9},{9,8},{10,11... | collective-permute-start | bytes 786440 | tf_op jit(solution)/shard_map/ppermute | solution.py:315
  87.1 14.7 %collective-permute-start.32 = (f32[16,4096]{1,0:T(8,128)S(1)}, f32[16,4096]{1,0:T(8,128)S(1)}, u32[]{:S(2)}, u32[]{:S(2)}) collective-permute-start(f32[16,4096]{1,0:T(8,128)S(1)} %collective-permute-done.30.refs_9_.refs_1_), channel_id=1, source_target_pairs={{0,1},{1,0},{2,3},{3,2},{4,5},{5,4},{6,7},{7,6},{8,9},{9,8},{10,11... | collective-permute-start | bytes 786440 | tf_op jit(solution)/shard_map/ppermute | solution.py:315
  89.0 7.1 %collective-permute-start.33 = (f32[10,8,512]{2,1,0:T(8,128)S(1)}, f32[10,8,512]{2,1,0:T(8,128)S(1)}, u32[]{:S(2)}, u32[]{:S(2)}) collective-permute-start(f32[10,8,512]{2,1,0:T(8,128)S(1)} %get-tuple-element.68), channel_id=1, source_target_pairs={{0,2},{2,0},{4,6},{6,4},{8,10},{10,8},{12,14},{14,12},{1,3},{3,1},... | collective-permute-start | bytes 491528 | tf_op jit(solution)/shard_map/ppermute | solution.py:315
  90.5 8.6 %collective-permute-start.34 = (f32[10,8,512]{2,1,0:T(8,128)S(1)}, f32[10,8,512]{2,1,0:T(8,128)S(1)}, u32[]{:S(2)}, u32[]{:S(2)}) collective-permute-start(f32[10,8,512]{2,1,0:T(8,128)S(1)} %get-tuple-element.69), channel_id=1, source_target_pairs={{0,4},{2,6},{4,0},{6,2},{8,12},{10,14},{12,8},{14,10},{1,5},{3,7},... | collective-permute-start | bytes 491528 | tf_op jit(solution)/shard_map/ppermute | solution.py:315
  92.1 16.0 %collective-permute-start.35 = (f32[10,8,512]{2,1,0:T(8,128)S(1)}, f32[10,8,512]{2,1,0:T(8,128)S(1)}, u32[]{:S(2)}, u32[]{:S(2)}) collective-permute-start(f32[10,8,512]{2,1,0:T(8,128)S(1)} %get-tuple-element.70), channel_id=1, source_target_pairs={{0,6},{2,4},{4,2},{6,0},{8,14},{10,12},{12,10},{14,8},{1,7},{3,5},... | collective-permute-start | bytes 491528 | tf_op jit(solution)/shard_map/ppermute | solution.py:315
  92.6 15.5 %collective-permute-start.36 = (f32[10,8,512]{2,1,0:T(8,128)S(1)}, f32[10,8,512]{2,1,0:T(8,128)S(1)}, u32[]{:S(2)}, u32[]{:S(2)}) collective-permute-start(f32[10,8,512]{2,1,0:T(8,128)S(1)} %get-tuple-element.71), channel_id=1, source_target_pairs={{0,8},{2,10},{4,12},{6,14},{8,0},{10,2},{12,4},{14,6},{1,9},{3,11}... | collective-permute-start | bytes 491528 | tf_op jit(solution)/shard_map/ppermute | solution.py:315
  96.2 11.9 %collective-permute-start.37 = (f32[10,8,512]{2,1,0:T(8,128)S(1)}, f32[10,8,512]{2,1,0:T(8,128)S(1)}, u32[]{:S(2)}, u32[]{:S(2)}) collective-permute-start(f32[10,8,512]{2,1,0:T(8,128)S(1)} %get-tuple-element.72), channel_id=1, source_target_pairs={{0,10},{2,8},{4,14},{6,12},{8,2},{10,0},{12,6},{14,4},{1,11},{3,9}... | collective-permute-start | bytes 491528 | tf_op jit(solution)/shard_map/ppermute | solution.py:315
  99.1 9.2 %collective-permute-start.38 = (f32[10,8,512]{2,1,0:T(8,128)S(1)}, f32[10,8,512]{2,1,0:T(8,128)S(1)}, u32[]{:S(2)}, u32[]{:S(2)}) collective-permute-start(f32[10,8,512]{2,1,0:T(8,128)S(1)} %get-tuple-element.73), channel_id=1, source_target_pairs={{0,12},{2,14},{4,8},{6,10},{8,4},{10,6},{12,0},{14,2},{1,13},{3,15... | collective-permute-start | bytes 491528 | tf_op jit(solution)/shard_map/ppermute | solution.py:315
  101.8 8.6 %collective-permute-start.39 = (f32[10,8,512]{2,1,0:T(8,128)S(1)}, f32[10,8,512]{2,1,0:T(8,128)S(1)}, u32[]{:S(2)}, u32[]{:S(2)}) collective-permute-start(f32[10,8,512]{2,1,0:T(8,128)S(1)} %get-tuple-element.74), channel_id=1, source_target_pairs={{0,14},{2,12},{4,10},{6,8},{8,6},{10,4},{12,2},{14,0},{1,15},{3,13... | collective-permute-start | bytes 491528 | tf_op jit(solution)/shard_map/ppermute | solution.py:315
